TPU v7x, 32 devices: a whole 2x2x4 slice. The times are simulated.
32 devices in a mesh: tok: 4 (over x, core), kv: 8 (over z, y).
Axes of the slice: x: 2, y: 2, z: 4, core: 2. Of those that a mesh axis runs over, the one named last changes fastest.
Arguments:
- queries: bfloat16 [4096, 768], P(('tok', 'kv')), may hold values from -36 to 36
- new_kv: bfloat16 [4096, 256], P(('tok', 'kv')), may hold values from -6 to 6
- segment_ids: int32 [4096], P(('tok', 'kv')), may hold values from 0 to 63, as said below
- prefix_len: int32 [64], P(('tok', 'kv')), may hold values from 0 to 4096, as said below
- page_table: int32 [32, 32], P(('tok', 'kv')), may hold values from 0 to 31, as said below
- cache: bfloat16 [1024, 128, 256], P(('tok', 'kv')), may hold values from -6 to 6
Outputs:
- attention: bfloat16 [4096, 768], P(('tok', 'kv'))
Inputs may be any that keep to these rules, and one draw needn't show every extreme that they name: `segment_ids`: device d's rows hold segments d * 2 to d * 2 + 1 in order, each on one row or more. Over each device's segments, the sum of ceil(prefix_len / 128) is at most 32; some device reaches it in every draw. page_table[d, k] for k // 8 = r lies in [r * 8, (r + 1) * 8); each such block of a row is a permutation of it; entries past the device's used pages are unused.
All inputs are finite; a program needn't handle non-finite values.
Results may differ from a plain program's by a relative error of at most 0.0085.
Values may be sent and summed in bfloat16 or wider, within the bound.
No kernel may reach another device: no remote copies, remote signals or barrier semaphores. Data moves between devices by JAX's collectives and lax.ppermute only.
A program may use at most 64 MiB of HBM per device.

v0:
```python
from functools import reduce

import jax
import jax.numpy as jnp
from jax import lax
from jax.sharding import PartitionSpec as P

HD = 128
HEADS = 6
PAGE = 128
REACH = 4
PPO = 8


NEGATIVE = -1e30


def from_behind(value, axis, steps):
    count = lax.axis_size(axis)
    pairs = [(source, (source + steps) % count) for source in range(count)]
    return lax.ppermute(value, axis, pairs)


def layout(lengths, table_row):
    page_total = table_row.shape[0]
    page_count = (lengths + PAGE - 1) // PAGE
    page_ends = jnp.cumsum(page_count)
    page_starts = page_ends - page_count
    page_number = jnp.arange(page_total, dtype=jnp.int32)
    page_seg = jnp.sum((page_number[:, None] >= page_ends[None, :]).astype(jnp.int32), axis=1)
    page_pick = page_seg[:, None] == jnp.arange(lengths.shape[0], dtype=jnp.int32)[None, :]
    first_page = jnp.sum(jnp.where(page_pick, page_starts[None, :], 0), axis=1)
    page_limit = jnp.sum(jnp.where(page_pick, lengths[None, :], 0), axis=1)
    positions = ((page_number - first_page) * PAGE)[:, None] + jnp.arange(PAGE, dtype=jnp.int32)[
        None, :
    ]
    usable = positions < page_limit[:, None]
    return (page_seg, usable)


def block_mask(local_seg, page_seg, usable, distance):
    lower = distance * PPO
    key_seg = jnp.repeat(page_seg[lower : lower + PPO], PAGE)
    key_ok = usable[lower : lower + PPO].reshape(PPO * PAGE)
    return (local_seg[:, None] == key_seg[None, :]) & key_ok[None, :]


def block_attention(query_rows, pair_rows, key_mask):
    row_count = query_rows.shape[0]
    query_heads = query_rows.reshape(row_count, HEADS, HD)
    scores = jnp.einsum(
        "rhd,kd->rhk", query_heads, pair_rows[:, :HD], preferred_element_type=jnp.float32
    ) * HD ** (-0.5)
    scores = jnp.where(key_mask[:, None, :], scores, NEGATIVE)
    maximum = jnp.max(scores, axis=2)
    weights = jnp.where(key_mask[:, None, :], jnp.exp(scores - maximum[:, :, None]), 0.0)
    weight_sum = jnp.sum(weights, axis=2)
    weighted = jnp.einsum(
        "rhk,kd->rhd",
        weights.astype(jnp.bfloat16),
        pair_rows[:, HD:],
        preferred_element_type=jnp.float32,
    )
    return (maximum, weight_sum, weighted)


def merge_partials(partials):
    maximum = reduce(jnp.maximum, [item[0] for item in partials])
    weight_sum = jnp.zeros_like(maximum)
    weighted = jnp.zeros_like(partials[0][2])
    for item in partials:
        factor = jnp.exp(item[0] - maximum)
        weight_sum = weight_sum + item[1] * factor
        weighted = weighted + item[2] * factor[:, :, None]
    row_count = weighted.shape[0]
    return (weighted / weight_sum[:, :, None]).reshape(row_count, HEADS * HD).astype(jnp.bfloat16)


def per_device(queries, new_kv, segment_ids, prefix_len, page_table, cache):
    row_count = queries.shape[0]
    local_seg = segment_ids - segment_ids[0]
    row_order = jnp.arange(row_count, dtype=jnp.int32)
    causal = (local_seg[:, None] == local_seg[None, :]) & (row_order[None, :] <= row_order[:, None])
    partials = [block_attention(queries, new_kv, causal)]
    table_row = page_table[0]
    page_seg, usable = layout(prefix_len, table_row)
    for distance in range(REACH):
        pool_block = cache[distance * PPO : (distance + 1) * PPO]
        if distance > 0:
            pool_block = from_behind(pool_block, ("tok", "kv"), -distance)
        slot_index = table_row[distance * PPO : (distance + 1) * PPO] - distance * PPO
        pair_rows = pool_block[slot_index].reshape(PPO * PAGE, 2 * HD)
        key_mask = block_mask(local_seg, page_seg, usable, distance)
        partials.append(block_attention(queries, pair_rows, key_mask))
    return merge_partials(partials)


def solution(mesh):
    placed = (
        P(("tok", "kv"), None),
        P(("tok", "kv"), None),
        P(("tok", "kv")),
        P(("tok", "kv")),
        P(("tok", "kv"), None),
        P(("tok", "kv"), None, None),
    )
    return jax.shard_map(
        per_device, mesh=mesh, in_specs=placed, out_specs=P(("tok", "kv"), None), check_vma=False
    )
```

profile of v0, /device:TPU:8, one launch (start us, length us, event | category | flops | bytes accessed | tf_op | source)
XLA Modules:
  0.0 75.7 jit_solution(3109590250832431905)
XLA Ops:
  0.0 0.0 copy-start.15
  0.0 0.0 copy-start.16
  0.0 2.8 %fusion.76 = (bf16[8,128,256]{2,1,0:T(8,128)(2,1)S(1)}, bf16[8,128,256]{2,1,0:T(8,128)(2,1)}, bf16[8,128,256]{2,1,0:T(8,128)(2,1)}, bf16[8,128,256]{2,1,0:T(8,128)(2,1)}) fusion(bf16[32,128,256]{2,1,0:T(8,128)(2,1)} %param.11), kind=kLoop, calls=%fused_computation.126 | loop fusion | bytes 4194304 | tf_op jit(solution)/shard_map/slice | solution.py:88
  2.8 1.4 %collective-permute-start = (bf16[8,128,256]{2,1,0:T(8,128)(2,1)}, bf16[8,128,256]{2,1,0:T(8,128)(2,1)}, u32[]{:S(2)}, u32[]{:S(2)}) collective-permute-start(bf16[8,128,256]{2,1,0:T(8,128)(2,1)} %get-tuple-element.14), channel_id=1, source_target_pairs={{0,31},{1,0},{2,1},{3,2},{4,3},{5,4},{6,5},{7,6},{8,7},{9,8},{10,9... | collective-permute-start | bytes 1572872 | tf_op jit(solution)/shard_map/ppermute | solution.py:21
  4.2 2.7 %collective-permute-start.2 = (bf16[8,128,256]{2,1,0:T(8,128)(2,1)}, bf16[8,128,256]{2,1,0:T(8,128)(2,1)}, u32[]{:S(2)}, u32[]{:S(2)}) collective-permute-start(bf16[8,128,256]{2,1,0:T(8,128)(2,1)} %get-tuple-element.15), channel_id=1, source_target_pairs={{0,29},{1,30},{2,31},{3,0},{4,1},{5,2},{6,3},{7,4},{8,5},{9,6},{10... | collective-permute-start | bytes 1572872 | tf_op jit(solution)/shard_map/ppermute | solution.py:21
  6.9 1.2 %collective-permute-start.1 = (bf16[8,128,256]{2,1,0:T(8,128)(2,1)}, bf16[8,128,256]{2,1,0:T(8,128)(2,1)}, u32[]{:S(2)}, u32[]{:S(2)}) collective-permute-start(bf16[8,128,256]{2,1,0:T(8,128)(2,1)} %get-tuple-element.16), channel_id=1, source_target_pairs={{0,30},{1,31},{2,0},{3,1},{4,2},{5,3},{6,4},{7,5},{8,6},{9,7},{10,... | collective-permute-start | bytes 1572872 | tf_op jit(solution)/shard_map/ppermute | solution.py:21
  8.2 0.0 copy-done.20
  8.2 0.0 copy-done.19
  8.3 0.2 reduce-window.8
  8.4 0.1 fusion.58
  8.5 0.1 fusion.77
  8.6 0.1 select_reduce_fusion.1
  8.7 0.0 copy-done.18
  8.7 0.1 fusion.59
  8.8 0.1 add_compare_fusion
  8.9 0.1 fusion.53
  9.0 0.0 copy-done.15
  9.0 0.2 copy.40
  9.2 0.1 broadcast_bitcast_fusion.2
  9.2 0.1 broadcast_bitcast_fusion
  9.3 1.4 %gather_fusion = bf16[8,128,256]{2,1,0:T(8,128)(2,1)} fusion(bf16[8,128,256]{2,1,0:T(8,128)(2,1)S(1)} %get-tuple-element.13, s32[1024]{0:T(1024)S(1)} %pad_clamp_fusion.3), kind=kCustom, calls=%fused_computation | custom fusion | bytes 1048608 | tf_op jit(solution)/shard_map/gather | solution.py:92
  10.7 0.0 copy-done.16
  10.7 0.2 fusion.78
  10.9 0.0 copy-start.4
  10.9 2.3 %compare_and_fusion.3 = (pred[128,1024]{0,1:T(8,128)(4,1)S(1)}, pred[128,1024]{0,1:T(8,128)(4,1)}, pred[128,1024]{0,1:T(8,128)(4,1)}, pred[128,1024]{0,1:T(8,128)(4,1)}) fusion(s32[128]{0:T(128)S(1)} %broadcast_subtract_fusion, s32[1024]{0:T(1024)S(1)} %get-tuple-element.46, pred[1024]{0:T(1024)(128)(4,1)S(1)} %get-tuple-element.17, ...), kind=kLoop, calls=%fused_computation.48 | loop fusion | flops 1048576 | bytes 545280 | tf_op jit(solution)/shard_map/and | solution.py:45
  13.3 1.5 %fusion = (f32[128,6]{0,1:T(8,128)S(1)}, f32[1024,128,6]{1,0,2:T(8,128)S(1)}) fusion(pred[128,1024]{0,1:T(8,128)(4,1)S(1)} %get-tuple-element.21, bf16[128,6,128]{0,2,1:T(8,128)(2,1)S(1)} %bitcast.147, bf16[1024,256]{1,0:T(8,128)(2,1)} %bitcast.151), kind=kOutput, calls=%fused_computation.12 | convolution fusion | flops 203685120 | bytes 3738624 | tf_op jit(solution)/shard_map/rhd,kd->rhk/dot_general | solution.py:51
  14.8 0.0 copy-done.4
  14.8 0.1 fusion.43
  14.9 0.8 %fusion.4 = f32[128,6]{0,1:T(8,128)S(1)} fusion(f32[1024,128,6]{1,0,2:T(8,128)S(1)} %get-tuple-element.40, f32[128,6]{0,1:T(8,128)S(1)} %get-tuple-element.39, pred[128,1024]{0,1:T(8,128)(4,1)S(1)} %get-tuple-element.21), kind=kLoop, calls=%fused_computation.16 | loop fusion | flops 3931392 | bytes 3282944 | tf_op jit(solution)/shard_map/reduce_sum | solution.py:57
  15.7 35.8 %collective-permute-done.1 = bf16[8,128,256]{2,1,0:T(8,128)(2,1)} collective-permute-done((bf16[8,128,256]{2,1,0:T(8,128)(2,1)}, bf16[8,128,256]{2,1,0:T(8,128)(2,1)}, u32[]{:S(2)}, u32[]{:S(2)}) %collective-permute-start.1) | collective-permute-done | bytes 524320 | tf_op jit(solution)/shard_map/ppermute | solution.py:21
  51.4 2.4 %gather_fusion.2 = bf16[8,128,256]{2,1,0:T(8,128)(2,1)} fusion(bf16[8,128,256]{2,1,0:T(8,128)(2,1)} %collective-permute-done.1, s32[1024]{0:T(1024)S(1)} %pad_clamp_fusion.1), kind=kCustom, calls=%fused_computation.2 | custom fusion | bytes 1048608 | tf_op jit(solution)/shard_map/gather | solution.py:92
  53.9 1.6 %fusion.2 = (f32[128,6]{0,1:T(8,128)S(1)}, f32[1024,128,6]{1,0,2:T(8,128)S(1)}) fusion(pred[128,1024]{0,1:T(8,128)(4,1)} %get-tuple-element.22, bf16[128,6,128]{0,2,1:T(8,128)(2,1)S(1)} %bitcast.148, bf16[1024,256]{1,0:T(8,128)(2,1)} %bitcast.153), kind=kOutput, calls=%fused_computation.14 | convolution fusion | flops 203685120 | bytes 3738624 | tf_op jit(solution)/shard_map/rhd,kd->rhk/dot_general | solution.py:51
  55.5 0.0 copy-start
  55.5 1.7 %copy-done = f32[1024,128,6]{1,0,2:T(8,128)} copy-done((f32[1024,128,6]{1,0,2:T(8,128)}, f32[1024,128,6]{1,0,2:T(8,128)S(1)}, u32[]{:S(2)}) %copy-start) | copy-done | bytes 3145752
  57.2 0.0 copy-done.7
  57.2 0.8 %fusion.8 = f32[128,6]{0,1:T(8,128)S(1)} fusion(f32[1024,128,6]{1,0,2:T(8,128)S(1)} %get-tuple-element.36, f32[128,6]{0,1:T(8,128)S(1)} %get-tuple-element.35, pred[128,1024]{0,1:T(8,128)(4,1)S(1)} %copy-done.7), kind=kLoop, calls=%fused_computation.20 | loop fusion | flops 3931392 | bytes 3282944 | tf_op jit(solution)/shard_map/reduce_sum | solution.py:57
  57.9 0.0 collective-permute-done.2
  57.9 2.5 %gather_fusion.3 = bf16[8,128,256]{2,1,0:T(8,128)(2,1)} fusion(bf16[8,128,256]{2,1,0:T(8,128)(2,1)} %collective-permute-done.2, s32[1024]{0:T(1024)S(1)} %pad_clamp_fusion), kind=kCustom, calls=%fused_computation.3 | custom fusion | bytes 1048608 | tf_op jit(solution)/shard_map/gather | solution.py:92
  60.4 1.6 %fusion.3 = (f32[128,6]{0,1:T(8,128)S(1)}, f32[1024,128,6]{1,0,2:T(8,128)S(1)}) fusion(pred[128,1024]{0,1:T(8,128)(4,1)} %get-tuple-element.23, bf16[128,6,128]{0,2,1:T(8,128)(2,1)S(1)} %bitcast.149, bf16[1024,256]{1,0:T(8,128)(2,1)} %bitcast.155), kind=kOutput, calls=%fused_computation.15 | convolution fusion | flops 203685120 | bytes 3738624 | tf_op jit(solution)/shard_map/rhd,kd->rhk/dot_general | solution.py:51
  62.0 0.0 copy-start.2
  62.0 1.7 %copy-done.2 = f32[1024,128,6]{1,0,2:T(8,128)} copy-done((f32[1024,128,6]{1,0,2:T(8,128)}, f32[1024,128,6]{1,0,2:T(8,128)S(1)}, u32[]{:S(2)}) %copy-start.2) | copy-done | bytes 3145752
  63.7 0.0 copy-done.9
  63.7 0.8 %fusion.10 = f32[128,6]{0,1:T(8,128)S(1)} fusion(f32[1024,128,6]{1,0,2:T(8,128)S(1)} %get-tuple-element.34, f32[128,6]{0,1:T(8,128)S(1)} %get-tuple-element.33, pred[128,1024]{0,1:T(8,128)(4,1)S(1)} %copy-done.9), kind=kLoop, calls=%fused_computation.22 | loop fusion | flops 3931392 | bytes 3282944 | tf_op jit(solution)/shard_map/reduce_sum | solution.py:57
  64.5 0.0 collective-permute-done
  64.5 2.4 %gather_fusion.1 = bf16[8,128,256]{2,1,0:T(8,128)(2,1)} fusion(bf16[8,128,256]{2,1,0:T(8,128)(2,1)} %collective-permute-done, s32[1024]{0:T(1024)S(1)} %pad_clamp_fusion.2), kind=kCustom, calls=%fused_computation.1 | custom fusion | bytes 1048608 | tf_op jit(solution)/shard_map/gather | solution.py:92
  66.9 1.7 %fusion.1 = (f32[128,6]{0,1:T(8,128)S(1)}, f32[1024,128,6]{1,0,2:T(8,128)S(1)}) fusion(pred[128,1024]{0,1:T(8,128)(4,1)} %get-tuple-element.24, bf16[128,6,128]{0,2,1:T(8,128)(2,1)S(1)} %bitcast.150, bf16[1024,256]{1,0:T(8,128)(2,1)} %bitcast.157), kind=kOutput, calls=%fused_computation.13 | convolution fusion | flops 203685120 | bytes 3738624 | tf_op jit(solution)/shard_map/rhd,kd->rhk/dot_general | solution.py:51
  68.7 0.0 copy-done.6
  68.7 0.8 %fusion.6 = f32[128,6]{0,1:T(8,128)S(1)} fusion(f32[1024,128,6]{1,0,2:T(8,128)S(1)} %get-tuple-element.38, f32[128,6]{0,1:T(8,128)S(1)} %get-tuple-element.37, pred[128,1024]{0,1:T(8,128)(4,1)S(1)} %copy-done.6), kind=kLoop, calls=%fused_computation.18 | loop fusion | flops 3931392 | bytes 3282944 | tf_op jit(solution)/shard_map/reduce_sum | solution.py:57
  69.5 0.0 copy-done.3
  69.5 0.0 copy-done.10
  69.5 0.0 copy-done.13
  69.5 0.0 copy-start.8
  69.5 0.0 copy-start.12
  69.5 0.9 %fusion.39 = f32[128,6,128]{0,2,1:T(8,128)S(1)} fusion(f32[1024,128,6]{1,0,2:T(8,128)S(1)} %copy-done.3, f32[128,6]{0,1:T(8,128)S(1)} %get-tuple-element.33, pred[128,1024]{0,1:T(8,128)(4,1)S(1)} %copy-done.10, bf16[1024,256]{1,0:T(8,128)(2,1)S(1)} %bitcast.156, f32[128,6]{0,1:T(8,128)S(1)} %get-tuple-element.12), kind=kOutput, calls=%fused_computation.43 | convolution fusion | flops 205357056 | bytes 3940352 | tf_op jit(solution)/shard_map/rhk,kd->rhd/dot_general | solution.py:58
  70.5 0.9 %copy-done.1 = f32[1024,128,6]{1,0,2:T(8,128)S(1)} copy-done((f32[1024,128,6]{1,0,2:T(8,128)S(1)}, f32[1024,128,6]{1,0,2:T(8,128)}, u32[]{:S(2)}) %copy-start.1) | copy-done | bytes 3145752
  71.4 0.1 copy-done.12
  71.5 0.9 %fusion.36 = f32[128,6,128]{0,2,1:T(8,128)S(1)} fusion(f32[1024,128,6]{1,0,2:T(8,128)S(1)} %copy-done.1, f32[128,6]{0,1:T(8,128)S(1)} %get-tuple-element.35, pred[128,1024]{0,1:T(8,128)(4,1)S(1)} %copy-done.8, bf16[1024,256]{1,0:T(8,128)(2,1)S(1)} %bitcast.154, f32[128,6]{0,1:T(8,128)S(1)} %get-tuple-element.11), kind=kOutput, calls=%fused_computation.42 | convolution fusion | flops 205357056 | bytes 3940352 | tf_op jit(solution)/shard_map/rhk,kd->rhd/dot_general | solution.py:58
  72.5 0.1 copy-done.14
  72.6 0.9 %fusion.33 = f32[128,6,128]{0,2,1:T(8,128)S(1)} fusion(f32[1024,128,6]{1,0,2:T(8,128)S(1)} %get-tuple-element.38, f32[128,6]{0,1:T(8,128)S(1)} %get-tuple-element.37, pred[128,1024]{0,1:T(8,128)(4,1)S(1)} %copy-done.6, bf16[1024,256]{1,0:T(8,128)(2,1)S(1)} %bitcast.158, f32[128,6]{0,1:T(8,128)S(1)} %get-tuple-element.10), kind=kOutput, calls=%fused_computation.41 | convolution fusion | flops 205357056 | bytes 3940352 | tf_op jit(solution)/shard_map/rhk,kd->rhd/dot_general | solution.py:58
  73.5 0.1 copy-done.11
  73.6 0.9 %fusion.30 = f32[128,6,128]{0,2,1:T(8,128)S(1)} fusion(f32[1024,128,6]{1,0,2:T(8,128)S(1)} %get-tuple-element.40, f32[128,6]{0,1:T(8,128)S(1)} %get-tuple-element.39, pred[128,1024]{0,1:T(8,128)(4,1)S(1)} %get-tuple-element.21, bf16[1024,256]{1,0:T(8,128)(2,1)S(1)} %bitcast.152, f32[128,6]{0,1:T(8,128)S(1)} %get-tuple-element.9), kind=kOutput, calls=%fused_computation.40 | convolution fusion | flops 205357056 | bytes 3940352 | tf_op jit(solution)/shard_map/rhk,kd->rhd/dot_general | solution.py:58
  74.6 0.1 copy-done.5
  74.6 0.3 fusion.42
  74.9 0.8 %copy.56 = bf16[128,768]{1,0:T(8,128)(2,1)} copy(bf16[128,768]{0,1:T(8,128)(2,1)S(1)} %bitcast.159) | data formatting | bytes 393216 | tf_op jit(solution)/shard_map/convert_element_type | solution.py:76
  (26 shorter events, 0.1 us)
Async XLA Ops:
  0.0 8.2 %copy-start.20 = (s32[128]{0:T(128)S(1)}, s32[128]{0:T(128)}, u32[]{:S(2)}) copy-start(s32[128]{0:T(128)} %param.8) | copy-start | bytes 1540
  0.0 8.2 %copy-start.19 = (s32[2]{0:T(128)S(1)}, s32[2]{0:T(128)}, u32[]{:S(2)}) copy-start(s32[2]{0:T(128)} %param.9) | copy-start | bytes 28
  0.0 8.7 %copy-start.18 = (s32[1,32]{1,0:T(1,128)S(1)}, s32[1,32]{1,0:T(1,128)}, u32[]{:S(2)}) copy-start(s32[1,32]{1,0:T(1,128)} %param.10) | copy-start | bytes 388
  0.0 9.0 %copy-start.15 = (bf16[128,768]{1,0:T(8,128)(2,1)S(1)}, bf16[128,768]{1,0:T(8,128)(2,1)}, u32[]{:S(2)}) copy-start(bf16[128,768]{1,0:T(8,128)(2,1)} %param.6) | copy-start | bytes 589828
  0.0 10.7 %copy-start.16 = (bf16[128,256]{1,0:T(8,128)(2,1)S(1)}, bf16[128,256]{1,0:T(8,128)(2,1)}, u32[]{:S(2)}) copy-start(bf16[128,256]{1,0:T(8,128)(2,1)} %param.7) | copy-start | bytes 196612
  2.8 61.7 %collective-permute-start = (bf16[8,128,256]{2,1,0:T(8,128)(2,1)}, bf16[8,128,256]{2,1,0:T(8,128)(2,1)}, u32[]{:S(2)}, u32[]{:S(2)}) collective-permute-start(bf16[8,128,256]{2,1,0:T(8,128)(2,1)} %get-tuple-element.14), channel_id=1, source_target_pairs={{0,31},{1,0},{2,1},{3,2},{4,3},{5,4},{6,5},{7,6},{8,7},{9,8},{10,9... | collective-permute-start | bytes 1572872 | tf_op jit(solution)/shard_map/ppermute | solution.py:21
  4.2 53.7 %collective-permute-start.2 = (bf16[8,128,256]{2,1,0:T(8,128)(2,1)}, bf16[8,128,256]{2,1,0:T(8,128)(2,1)}, u32[]{:S(2)}, u32[]{:S(2)}) collective-permute-start(bf16[8,128,256]{2,1,0:T(8,128)(2,1)} %get-tuple-element.15), channel_id=1, source_target_pairs={{0,29},{1,30},{2,31},{3,0},{4,1},{5,2},{6,3},{7,4},{8,5},{9,6},{10... | collective-permute-start | bytes 1572872 | tf_op jit(solution)/shard_map/ppermute | solution.py:21
  6.9 44.5 %collective-permute-start.1 = (bf16[8,128,256]{2,1,0:T(8,128)(2,1)}, bf16[8,128,256]{2,1,0:T(8,128)(2,1)}, u32[]{:S(2)}, u32[]{:S(2)}) collective-permute-start(bf16[8,128,256]{2,1,0:T(8,128)(2,1)} %get-tuple-element.16), channel_id=1, source_target_pairs={{0,30},{1,31},{2,0},{3,1},{4,2},{5,3},{6,4},{7,5},{8,6},{9,7},{10,... | collective-permute-start | bytes 1572872 | tf_op jit(solution)/shard_map/ppermute | solution.py:21
  10.9 3.9 %copy-start.4 = (f32[128,6,128]{0,2,1:T(8,128)}, f32[128,6,128]{0,2,1:T(8,128)S(1)}, u32[]{:S(2)}) copy-start(f32[128,6,128]{0,2,1:T(8,128)S(1)} %get-tuple-element.42) | copy-start | bytes 1179652
  53.9 3.3 %copy-start.7 = (pred[128,1024]{0,1:T(8,128)(4,1)S(1)}, pred[128,1024]{0,1:T(8,128)(4,1)}, u32[]{:S(2)}) copy-start(pred[128,1024]{0,1:T(8,128)(4,1)} %get-tuple-element.22) | copy-start | bytes 393220
  55.5 1.7 %copy-start = (f32[1024,128,6]{1,0,2:T(8,128)}, f32[1024,128,6]{1,0,2:T(8,128)S(1)}, u32[]{:S(2)}) copy-start(f32[1024,128,6]{1,0,2:T(8,128)S(1)} %get-tuple-element.36) | copy-start | bytes 9437188
  60.4 3.3 %copy-start.9 = (pred[128,1024]{0,1:T(8,128)(4,1)S(1)}, pred[128,1024]{0,1:T(8,128)(4,1)}, u32[]{:S(2)}) copy-start(pred[128,1024]{0,1:T(8,128)(4,1)} %get-tuple-element.23) | copy-start | bytes 393220
  62.0 1.7 %copy-start.2 = (f32[1024,128,6]{1,0,2:T(8,128)}, f32[1024,128,6]{1,0,2:T(8,128)S(1)}, u32[]{:S(2)}) copy-start(f32[1024,128,6]{1,0,2:T(8,128)S(1)} %get-tuple-element.34) | copy-start | bytes 9437188
  66.9 1.8 %copy-start.6 = (pred[128,1024]{0,1:T(8,128)(4,1)S(1)}, pred[128,1024]{0,1:T(8,128)(4,1)}, u32[]{:S(2)}) copy-start(pred[128,1024]{0,1:T(8,128)(4,1)} %get-tuple-element.24) | copy-start | bytes 393220
  66.9 2.6 %copy-start.3 = (f32[1024,128,6]{1,0,2:T(8,128)S(1)}, f32[1024,128,6]{1,0,2:T(8,128)}, u32[]{:S(2)}) copy-start(f32[1024,128,6]{1,0,2:T(8,128)} %copy-done.2) | copy-start | bytes 9437188
  66.9 2.6 %copy-start.10 = (pred[128,1024]{0,1:T(8,128)(4,1)S(1)}, pred[128,1024]{0,1:T(8,128)(4,1)}, u32[]{:S(2)}) copy-start(pred[128,1024]{0,1:T(8,128)(4,1)} %get-tuple-element.23) | copy-start | bytes 393220
  66.9 2.6 %copy-start.13 = (bf16[8,128,256]{2,1,0:T(8,128)(2,1)S(1)}, bf16[8,128,256]{2,1,0:T(8,128)(2,1)}, u32[]{:S(2)}) copy-start(bf16[8,128,256]{2,1,0:T(8,128)(2,1)} %gather_fusion.3) | copy-start | bytes 1572868
  69.5 1.9 %copy-start.1 = (f32[1024,128,6]{1,0,2:T(8,128)S(1)}, f32[1024,128,6]{1,0,2:T(8,128)}, u32[]{:S(2)}) copy-start(f32[1024,128,6]{1,0,2:T(8,128)} %copy-done) | copy-start | bytes 9437188
  69.5 1.9 %copy-start.8 = (pred[128,1024]{0,1:T(8,128)(4,1)S(1)}, pred[128,1024]{0,1:T(8,128)(4,1)}, u32[]{:S(2)}) copy-start(pred[128,1024]{0,1:T(8,128)(4,1)} %get-tuple-element.22) | copy-start | bytes 393220
  69.5 2.0 %copy-start.12 = (bf16[8,128,256]{2,1,0:T(8,128)(2,1)S(1)}, bf16[8,128,256]{2,1,0:T(8,128)(2,1)}, u32[]{:S(2)}) copy-start(bf16[8,128,256]{2,1,0:T(8,128)(2,1)} %gather_fusion.2) | copy-start | bytes 1572868
  71.5 1.0 %copy-start.14 = (bf16[8,128,256]{2,1,0:T(8,128)(2,1)S(1)}, bf16[8,128,256]{2,1,0:T(8,128)(2,1)}, u32[]{:S(2)}) copy-start(bf16[8,128,256]{2,1,0:T(8,128)(2,1)} %gather_fusion.1) | copy-start | bytes 1572868
  72.6 1.0 %copy-start.11 = (bf16[8,128,256]{2,1,0:T(8,128)(2,1)S(1)}, bf16[8,128,256]{2,1,0:T(8,128)(2,1)}, u32[]{:S(2)}) copy-start(bf16[8,128,256]{2,1,0:T(8,128)(2,1)} %gather_fusion) | copy-start | bytes 1572868
  73.6 1.0 %copy-start.5 = (f32[128,6,128]{0,2,1:T(8,128)S(1)}, f32[128,6,128]{0,2,1:T(8,128)}, u32[]{:S(2)}) copy-start(f32[128,6,128]{0,2,1:T(8,128)} %copy-done.4) | copy-start | bytes 1179652
  73.6 1.0 %copy-start.17 = (bf16[128,256]{1,0:T(8,128)(2,1)S(1)}, bf16[128,256]{1,0:T(8,128)(2,1)}, u32[]{:S(2)}) copy-start(bf16[128,256]{1,0:T(8,128)(2,1)} %param.7) | copy-start | bytes 196612
where the time goes:
time: 76.2 us; the launch traced here: 75.7 us
  waiting for transfers between devices  35.8 us (47%)
  local copies, waits for them, and re-layouts  17.4 us (23%)
  matrix products  10.8 us (14%)
  other arithmetic  6.14 us (8%)
  starting transfers between devices  5.38 us (7%)
    ppermute x3, waiting for transfers between devices, from_behind(): return lax.ppermute(value, axis, pairs)  35.8 us
    gather x4, local copies, waits for them, and re-layouts, per_device(): pair_rows = pool_block[slot_index].reshape(PPO * PAGE, 2 * HD)  8.7 us
    dot_general x5, matrix products, block_attention(): jnp.einsum('rhd,kd->rhk', query_heads, pair_rows[:, :HD], preferred_eleme...  6.71 us
    ppermute x3, starting transfers between devices, from_behind(): return lax.ppermute(value, axis, pairs)  5.38 us
    unnamed x43, local copies, waits for them, and re-layouts  4.84 us
    dot_general x5, matrix products, block_attention(): jnp.einsum('rhk,kd->rhd', weights.astype(jnp.bfloat16), pair_rows[:, HD:]...  4.05 us
    reduce_sum x5, other arithmetic, block_attention(): weight_sum = jnp.sum(weights, axis=2)  3.13 us
    slice x1, local copies, waits for them, and re-layouts, per_device(): pool_block = cache[distance * PPO:(distance + 1) * PPO]  2.77 us
  transfers between devices with their start and end apart: 3, of which 1 were waited for; matrix products, arithmetic and copies ran while one was open for 22% of the time, Pallas kernels for 0%

commit v1 on v0

v1 whole, which is shorter than its diff:
```python
import functools

import jax
import jax.numpy as jnp
from jax import lax
from jax.experimental import pallas as pl
from jax.experimental.pallas import tpu as pltpu
from jax.sharding import PartitionSpec as P

HD = 128
HEADS = 6
PAGE = 128
REACH = 4
PPO = 8
LONG = 1
ROWS = 128
WIDTH = HEADS * HD
STAT_ROWS = 8
NEGATIVE = -1e30
SCALE2 = HD**-0.5 * 1.4426950408889634
AXES = ("tok", "kv")
CUT, PARITY = REACH, REACH + 1


def iota(axis, shape=(ROWS, PAGE)):
    return lax.broadcasted_iota(jnp.int32, shape, axis)


def fact(q_ref, tile):
    return q_ref[ROWS:, tile * PAGE : (tile + 1) * PAGE].astype(jnp.float32)


def block_keys(q_ref, pages, block):
    row, lane = iota(0).astype(jnp.float32), iota(1).astype(jnp.float32)
    first = row < fact(q_ref, CUT)[:1]
    counts = fact(q_ref, block)
    bias = []
    for slot in range(PPO):
        count = counts[slot : slot + 1]
        bias.append(jnp.where(lane < jnp.where(first, count, -count), 0.0, NEGATIVE))
    flat = pages[...].reshape(PPO * PAGE, 2 * HD)
    return flat[:, :HD], flat[:, HD:], jnp.concatenate(bias, 1)


def pack_kernel(length_hbm, table_hbm, segment_hbm, q_hbm, cache_hbm, out_ref, swap_ref, lengths, table, segments, sems):
    ends = [
        (segment_hbm, segments),
        (length_hbm, lengths),
        (table_hbm, table),
        (q_hbm, out_ref.at[:ROWS]),
        (cache_hbm.at[PPO : 2 * PPO], swap_ref),
    ]
    copies = [pltpu.make_async_copy(source, target, sems.at[i]) for i, (source, target) in enumerate(ends)]
    for copy in copies:
        copy.start()
    odd = jnp.bitwise_and(lax.axis_index("kv"), 1)
    odd = jnp.full((STAT_ROWS, PAGE), odd, jnp.int32).astype(jnp.float32)
    out_ref[ROWS:, PARITY * PAGE : (PARITY + 1) * PAGE] = odd.astype(jnp.bfloat16)
    for copy in copies[:3]:
        copy.wait()
    last = jnp.int32(0)
    for bit in (64, 32, 16, 8, 4, 2, 1):
        last = jnp.where(segments[last + bit] == segments[0], last + bit, last)
    cut = jnp.full((STAT_ROWS, PAGE), last + 1, jnp.int32).astype(jnp.float32)
    out_ref[ROWS:, CUT * PAGE : (CUT + 1) * PAGE] = cut.astype(jnp.bfloat16)
    count0 = lax.shift_right_logical(lengths[0] + (PAGE - 1), 7)
    slot_row = iota(0, (STAT_ROWS, PAGE))
    for block in range(REACH):
        tile = jnp.zeros((STAT_ROWS, PAGE), jnp.int32)
        for k in range(block * PPO, (block + 1) * PPO):
            left0 = jnp.clip(lengths[0] - k * PAGE, 0, PAGE)
            left1 = jnp.clip(lengths[1] - (k - count0) * PAGE, 0, PAGE)
            left = jnp.where(k < count0, left0, -left1)
            tile = jnp.where(slot_row == jnp.bitwise_and(table[0, k], PPO - 1), left, tile)
        out_ref[ROWS:, block * PAGE : (block + 1) * PAGE] = tile.astype(jnp.float32).astype(jnp.bfloat16)
    for copy in copies[3:]:
        copy.wait()


def attend(query, keys, values, bias):
    s = lax.dot_general(query, keys, (((1,), (1,)), ((), ())), preferred_element_type=jnp.float32)
    s = s * SCALE2 + bias
    top = jnp.max(s, axis=1, keepdims=True)
    w = jnp.exp2(s - top)
    total = jnp.sum(w, axis=1, keepdims=True)
    out = jnp.dot(w.astype(jnp.bfloat16), values, preferred_element_type=jnp.float32)
    return out, top, total


def join(a, b):
    top = jnp.maximum(a[1], b[1])
    fa, fb = jnp.exp2(a[1] - top), jnp.exp2(b[1] - top)
    return a[0] * fa + b[0] * fb, top, a[2] * fa + b[2] * fb


def head(x, h):
    return x[:ROWS, h * HD : (h + 1) * HD]


def columns(cols):
    lane = iota(1)
    out = jnp.zeros((ROWS, PAGE), jnp.float32)
    for i, col in enumerate(cols):
        out = jnp.where(lane == i, col, out)
    return out


def write_payload(out_ref, parts):
    for h, (o, top, total) in enumerate(parts):
        out_ref[:ROWS, h * HD : (h + 1) * HD] = (o / total).astype(jnp.bfloat16)
    lse = columns([top + jnp.log2(total) for _, top, total in parts]).T[:STAT_ROWS]
    left = lse
    for i in range(3):
        term = left.astype(jnp.bfloat16)
        out_ref[ROWS:, i * HD : (i + 1) * HD] = term
        left = left - term.astype(jnp.float32)
    out_ref[ROWS:, 3 * HD :] = jnp.zeros((STAT_ROWS, WIDTH - 3 * HD), jnp.bfloat16)


def write_partial(out_ref, lse_ref, parts):
    for h, (o, _, total) in enumerate(parts):
        out_ref[:, h * HD : (h + 1) * HD] = o / total
    lse_ref[...] = columns([top + jnp.log2(total) for _, top, total in parts])


def payload_lse(ref):
    lse = jnp.zeros((STAT_ROWS, PAGE), jnp.float32)
    for i in (2, 1, 0):
        lse = lse + ref[ROWS:, i * HD : (i + 1) * HD].astype(jnp.float32)
    full = jnp.concatenate([lse, jnp.zeros((ROWS - STAT_ROWS, PAGE), jnp.float32)], 0)
    return full.T


def block_parts(q_ref, pages, block):
    keys, values, bias = block_keys(q_ref, pages, block)
    return [attend(head(q_ref, h), keys, values, bias) for h in range(HEADS)]


def near_kernel(q_ref, kv_ref, page_ref, out_ref, lse_ref):
    keys, values, bias = block_keys(q_ref, page_ref, 0)
    row, lane = iota(0), iota(1)
    cut = fact(q_ref, CUT)[:1]
    same = (lane <= row) & ((lane.astype(jnp.float32) >= cut) | (row.astype(jnp.float32) < cut))
    keys = jnp.concatenate([kv_ref[:, :HD], keys], 0)
    values = jnp.concatenate([kv_ref[:, HD:], values], 0)
    bias = jnp.concatenate([jnp.where(same, 0.0, NEGATIVE), bias], 1)
    write_partial(out_ref, lse_ref, [attend(head(q_ref, h), keys, values, bias) for h in range(HEADS)])


def far_kernel(q_ref, page_ref, out_ref):
    write_payload(out_ref, block_parts(q_ref, page_ref, 3))


def middle_kernel(q_ref, page_ref, out_ref, lse_ref):
    write_partial(out_ref, lse_ref, block_parts(q_ref, page_ref, 2))


def swap_parts(parity, q_ref, swap_ref, part_ref, part_lse_ref):
    keys, values, bias = block_keys(q_ref, swap_ref, 1)
    bias = bias + jnp.where(fact(q_ref, PARITY)[:1, :1] == parity, 0.0, NEGATIVE)
    parts = []
    for h in range(HEADS):
        part = part_ref[:, h * HD : (h + 1) * HD], part_lse_ref[:, h : h + 1], 1.0
        parts.append(join(part, attend(head(q_ref, h), keys, values, bias)))
    return parts


def both_kernel(q_ref, swap_ref, part_ref, part_lse_ref, out_ref):
    write_payload(out_ref, swap_parts(1.0, q_ref, swap_ref, part_ref, part_lse_ref))


def own_kernel(q_ref, swap_ref, part_ref, part_lse_ref, out_ref, lse_ref):
    write_partial(out_ref, lse_ref, swap_parts(0.0, q_ref, swap_ref, part_ref, part_lse_ref))


def final_kernel(own_ref, own_lse_ref, two_ref, three_ref, out_ref):
    refs = (own_ref, two_ref, three_ref)
    lses = [own_lse_ref[...], payload_lse(two_ref), payload_lse(three_ref)]
    top = functools.reduce(jnp.maximum, lses)
    shares = [jnp.exp2(x - top) for x in lses]
    total = sum(shares)
    shares = [x / total for x in shares]
    for h in range(HEADS):
        span = slice(h * HD, (h + 1) * HD)
        out = 0.0
        for ref, share in zip(refs, shares):
            out = out + ref[:ROWS, span].astype(jnp.float32) * share[:, h : h + 1]
        out_ref[:, span] = out.astype(jnp.bfloat16)


SMEM = pl.BlockSpec(memory_space=pltpu.SMEM)
VMEM = pl.BlockSpec(memory_space=pltpu.VMEM)


FULL = jax.ShapeDtypeStruct((ROWS, WIDTH), jnp.float32)
LSE = jax.ShapeDtypeStruct((ROWS, PAGE), jnp.float32)
SENT = jax.ShapeDtypeStruct((ROWS + STAT_ROWS, WIDTH), jnp.bfloat16)
RESULT = jax.ShapeDtypeStruct((ROWS, WIDTH), jnp.bfloat16)


def cost(keys):
    return pl.CostEstimate(
        flops=4 * ROWS * HEADS * keys * HD,
        bytes_accessed=4 * keys * HD + 4 * ROWS * WIDTH,
        transcendentals=ROWS * HEADS * keys,
    )


PARAMS = pltpu.CompilerParams(vmem_limit_bytes=16 << 20)


def call(body, name, keys, out_shape, *arrays):
    return pl.pallas_call(
        body,
        in_specs=[VMEM] * len(arrays),
        out_specs=jax.tree.map(lambda _: VMEM, out_shape),
        out_shape=out_shape,
        compiler_params=PARAMS,
        cost_estimate=cost(keys),
        name=name,
    )(*arrays)


def shift(value, steps, count):
    return lax.ppermute(value, AXES, [(s, (s + steps) % count) for s in range(count)])


def after(value, *others):
    return lax.optimization_barrier((value, *others))[0]


def per_device(queries, new_kv, segment_ids, prefix_len, page_table, cache):
    count = lax.axis_size(AXES)
    packed, sent1 = pl.pallas_call(
        pack_kernel,
        in_specs=[pl.BlockSpec(memory_space=pltpu.HBM)] * 5,
        out_specs=[VMEM, VMEM],
        out_shape=[SENT, jax.ShapeDtypeStruct((PPO, PAGE, 2 * HD), jnp.bfloat16)],
        scratch_shapes=[
            pltpu.SMEM(prefix_len.shape, jnp.int32),
            pltpu.SMEM(page_table.shape, jnp.int32),
            pltpu.SMEM(segment_ids.shape, jnp.int32),
            pltpu.SemaphoreType.DMA((5,)),
        ],
        compiler_params=pltpu.CompilerParams(vmem_limit_bytes=(65536 - 1700) << 10),
        cost_estimate=cost(16),
        name="pack",
    )(prefix_len, page_table, segment_ids, queries, cache)
    q3 = shift(packed, 3, count)
    q2 = shift(packed, 2, count)
    swapped = lax.ppermute(sent1, AXES, [(s, s ^ 1) for s in range(count)])
    pool = after(cache, packed)
    blocks = [pool[i * PPO : (i + 1) * PPO] for i in range(REACH)]

    two = call(middle_kernel, "middle", 1024 * LONG, (FULL, LSE), q2, blocks[2])
    far = call(far_kernel, "far", 1024 * LONG, SENT, q3, after(blocks[3], two[1]))
    back3 = shift(far, -3, count)
    both = call(both_kernel, "both", 1024, SENT, q2, after(swapped, far), *two)
    back2 = shift(both, -2, count)
    near = call(near_kernel, "near", 1152, (FULL, LSE), packed, new_kv, blocks[0])
    own = call(own_kernel, "own", 1024, (FULL, LSE), packed, swapped, *near)
    return call(final_kernel, "final", 16, RESULT, *own, back2, back3)


def solution(mesh):
    placed = (
        P(AXES, None),
        P(AXES, None),
        P(AXES),
        P(AXES),
        P(AXES, None),
        P(AXES, None, None),
    )
    return jax.shard_map(per_device, mesh=mesh, in_specs=placed, out_specs=P(AXES, None), check_vma=False)
```

time: 76.2 us -> 40.4 us (0.53)
  the two profiles are of different devices: /device:TPU:8 before, /device:TPU:0 now
where the time goes in v1:
time: 40.4 us; the launch traced here: 40.2 us
  Pallas kernels  16.4 us (41%)
  waiting for transfers between devices  16.1 us (40%)
  starting transfers between devices  6.22 us (15%)
  local copies, waits for them, and re-layouts  1.47 us (4%)
    ppermute x4, waiting for transfers between devices, shift(): lax.ppermute(value, AXES, [(s, (s + steps) % count) for s in range(count)])  16.1 us
    pallas_call x6, Pallas kernels, call(): pl.pallas_call(body, in_specs=[VMEM] * len(arrays), out_specs=jax.tree.ma...  14.3 us
    ppermute x4, starting transfers between devices, shift(): lax.ppermute(value, AXES, [(s, (s + steps) % count) for s in range(count)])  3.19 us
    ppermute x1, starting transfers between devices, per_device(): swapped = lax.ppermute(sent1, AXES, [(s, s ^ 1) for s in range(count)])  3.03 us
    pallas_call x1, Pallas kernels, per_device(): pl.pallas_call(pack_kernel, in_specs=[pl.BlockSpec(memory_space=pltpu.HBM...  2.08 us
    slice x1, local copies, waits for them, and re-layouts, per_device(): blocks = [pool[i * PPO:(i + 1) * PPO] for i in range(REACH)]  1.46 us
  transfers between devices with their start and end apart: 5, of which 3 were waited for; matrix products, arithmetic and copies ran while one was open for 4% of the time, Pallas kernels for 32%

profile of v1, /device:TPU:0, one launch (start us, length us, event | category | flops | bytes accessed | tf_op | source)
XLA Modules:
  0.0 40.2 jit_solution(2408165251985907078)
XLA Ops:
  0.0 2.1 %pack.1 = (bf16[136,768]{1,0:T(8,128)(2,1)}, bf16[8,128,256]{2,1,0:T(8,128)(2,1)}) custom-call(s32[2]{0:T(128)} %length_hbm.1, s32[1,32]{1,0:T(1,128)} %table_hbm.1, s32[128]{0:T(128)} %segment_hbm.1, bf16[128,768]{1,0:T(8,128)(2,1)} %q_hbm.1, bf16[32,128,256]{2,1,0:T(8,128)(2,1)} %cache_hbm.1), custom_call_target="tpu_custom_call" | custom-call | flops 6291456 | bytes 401408 | tf_op jit(solution)/shard_map/pack/pallas_call | solution.py:234
  2.1 3.0 %collective-permute-start = (bf16[8,128,256]{2,1,0:T(8,128)(2,1)}, bf16[8,128,256]{2,1,0:T(8,128)(2,1)S(1)}, u32[]{:S(2)}, u32[]{:S(2)}) collective-permute-start(bf16[8,128,256]{2,1,0:T(8,128)(2,1)} %get-tuple-element.17), channel_id=1, source_target_pairs={{0,1},{1,0},{2,3},{3,2},{4,5},{5,4},{6,7},{7,6},{8,9},{9,8},{10,11... | collective-permute-start | bytes 1572872 | tf_op jit(solution)/shard_map/ppermute | solution.py:251
  5.1 1.6 %collective-permute-start.1 = (bf16[136,768]{1,0:T(8,128)(2,1)}, bf16[136,768]{1,0:T(8,128)(2,1)S(1)}, u32[]{:S(2)}, u32[]{:S(2)}) collective-permute-start(bf16[136,768]{1,0:T(8,128)(2,1)} %get-tuple-element.16.q_ref), channel_id=1, source_target_pairs={{0,2},{1,3},{2,4},{3,5},{4,6},{5,7},{6,8},{7,9},{8,10},{9,11},{10,... | collective-permute-start | bytes 626696 | tf_op jit(solution)/shard_map/ppermute | solution.py:225
  6.7 1.5 %collective-permute-start.2 = (bf16[136,768]{1,0:T(8,128)(2,1)}, bf16[136,768]{1,0:T(8,128)(2,1)S(1)}, u32[]{:S(2)}, u32[]{:S(2)}) collective-permute-start(bf16[136,768]{1,0:T(8,128)(2,1)} %get-tuple-element.16.q_ref), channel_id=1, source_target_pairs={{0,3},{1,4},{2,5},{3,6},{4,7},{5,8},{6,9},{7,10},{8,11},{9,12},{10... | collective-permute-start | bytes 626696 | tf_op jit(solution)/shard_map/ppermute | solution.py:225
  8.2 1.5 %fusion = (bf16[8,128,256]{2,1,0:T(8,128)(2,1)S(1)}, bf16[8,128,256]{2,1,0:T(8,128)(2,1)S(1)}, bf16[8,128,256]{2,1,0:T(8,128)(2,1)S(1)}) fusion(bf16[32,128,256]{2,1,0:T(8,128)(2,1)} %cache_hbm.1), kind=kLoop, calls=%fused_computation | loop fusion | bytes 3145728 | tf_op jit(solution)/shard_map/slice | solution.py:253
  9.7 5.5 %collective-permute-done.1.q_ref = bf16[136,768]{1,0:T(8,128)(2,1)S(1)} collective-permute-done((bf16[136,768]{1,0:T(8,128)(2,1)}, bf16[136,768]{1,0:T(8,128)(2,1)S(1)}, u32[]{:S(2)}, u32[]{:S(2)}) %collective-permute-start.1) | collective-permute-done | bytes 208928 | tf_op jit(solution)/shard_map/ppermute | solution.py:225
  15.2 0.0 copy-start
  15.2 0.0 copy-start.1
  15.2 2.2 %middle.1 = (f32[128,768]{1,0:T(8,128)S(1)}, f32[128,128]{1,0:T(8,128)S(1)}) custom-call(bf16[136,768]{1,0:T(8,128)(2,1)S(1)} %collective-permute-done.1.q_ref, bf16[8,128,256]{2,1,0:T(8,128)(2,1)S(1)} %get-tuple-element.27.page_ref), custom_call_target="tpu_custom_call" | custom-call | flops 402653184 | bytes 917504 | tf_op jit(solution)/shard_map/middle/pallas_call | solution.py:213
  17.4 6.5 %collective-permute-done.2.q_ref = bf16[136,768]{1,0:T(8,128)(2,1)S(1)} collective-permute-done((bf16[136,768]{1,0:T(8,128)(2,1)}, bf16[136,768]{1,0:T(8,128)(2,1)S(1)}, u32[]{:S(2)}, u32[]{:S(2)}) %collective-permute-start.2) | collective-permute-done | bytes 208928 | tf_op jit(solution)/shard_map/ppermute | solution.py:225
  24.0 2.2 %far.1 = bf16[136,768]{1,0:T(8,128)(2,1)S(1)} custom-call(bf16[136,768]{1,0:T(8,128)(2,1)S(1)} %collective-permute-done.2.q_ref, bf16[8,128,256]{2,1,0:T(8,128)(2,1)S(1)} %get-tuple-element.24.page_ref), custom_call_target="tpu_custom_call" | custom-call | flops 402653184 | bytes 917504 | tf_op jit(solution)/shard_map/far/pallas_call | solution.py:213
  26.2 0.1 collective-permute-start.4
  26.3 0.0 collective-permute-done.swap_ref
  26.3 3.1 %both.1 = bf16[136,768]{1,0:T(8,128)(2,1)S(1)} custom-call(bf16[136,768]{1,0:T(8,128)(2,1)S(1)} %collective-permute-done.1.q_ref, bf16[8,128,256]{2,1,0:T(8,128)(2,1)S(1)} %collective-permute-done.swap_ref, f32[128,768]{1,0:T(8,128)S(1)} %get-tuple-element.26.part_ref, f32[128,128]{1,0:T(8,128)S(1)} %get-tuple-element.23.part_lse_ref), custom_call_target="tpu_custom_call" | custom-call | flops 402653184 | bytes 917504 | tf_op jit(solution)/shard_map/both/pallas_call | solution.py:213
  29.4 0.0 collective-permute-start.3
  29.4 0.0 copy-done
  29.4 0.0 copy-done.1
  29.4 2.5 %near.1 = (f32[128,768]{1,0:T(8,128)S(1)}, f32[128,128]{1,0:T(8,128)S(1)}) custom-call(bf16[136,768]{1,0:T(8,128)(2,1)S(1)} %copy-done, bf16[128,256]{1,0:T(8,128)(2,1)S(1)} %copy-done.1, bf16[8,128,256]{2,1,0:T(8,128)(2,1)S(1)} %get-tuple-element.29.page_ref), custom_call_target="tpu_custom_call" | custom-call | flops 452984832 | bytes 983040 | tf_op jit(solution)/shard_map/near/pallas_call | solution.py:213
  32.0 3.0 %own.1 = (f32[128,768]{1,0:T(8,128)S(1)}, f32[128,128]{1,0:T(8,128)S(1)}) custom-call(bf16[136,768]{1,0:T(8,128)(2,1)S(1)} %copy-done, bf16[8,128,256]{2,1,0:T(8,128)(2,1)S(1)} %collective-permute-done.swap_ref, f32[128,768]{1,0:T(8,128)S(1)} %get-tuple-element.19.part_ref, f32[128,128]{1,0:T(8,128)S(1)} %get-tuple-element.20.part_lse_ref), custom_call_target="tpu_custom_call" | custom-call | flops 402653184 | bytes 917504 | tf_op jit(solution)/shard_map/own/pallas_call | solution.py:213
  34.9 0.0 collective-permute-done.4.three_ref
  35.0 4.0 %collective-permute-done.3.two_ref = bf16[136,768]{1,0:T(8,128)(2,1)S(1)} collective-permute-done((bf16[136,768]{1,0:T(8,128)(2,1)S(1)}, bf16[136,768]{1,0:T(8,128)(2,1)S(1)}, u32[]{:S(2)}, u32[]{:S(2)}) %collective-permute-start.3) | collective-permute-done | bytes 208928 | tf_op jit(solution)/shard_map/ppermute | solution.py:225
  39.0 1.2 %final.1 = bf16[128,768]{1,0:T(8,128)(2,1)} custom-call(f32[128,768]{1,0:T(8,128)S(1)} %get-tuple-element.21.own_ref, f32[128,128]{1,0:T(8,128)S(1)} %get-tuple-element.22.own_lse_ref, bf16[136,768]{1,0:T(8,128)(2,1)S(1)} %collective-permute-done.3.two_ref, bf16[136,768]{1,0:T(8,128)(2,1)S(1)} %collective-permute-done.4.three_ref), custom_call_target="tpu_custom_call" | custom-call | flops 6291456 | bytes 401408 | tf_op jit(solution)/shard_map/final/pallas_call | solution.py:213
Async XLA Ops:
  2.1 24.2 %collective-permute-start = (bf16[8,128,256]{2,1,0:T(8,128)(2,1)}, bf16[8,128,256]{2,1,0:T(8,128)(2,1)S(1)}, u32[]{:S(2)}, u32[]{:S(2)}) collective-permute-start(bf16[8,128,256]{2,1,0:T(8,128)(2,1)} %get-tuple-element.17), channel_id=1, source_target_pairs={{0,1},{1,0},{2,3},{3,2},{4,5},{5,4},{6,7},{7,6},{8,9},{9,8},{10,11... | collective-permute-start | bytes 1572872 | tf_op jit(solution)/shard_map/ppermute | solution.py:251
  5.1 10.1 %collective-permute-start.1 = (bf16[136,768]{1,0:T(8,128)(2,1)}, bf16[136,768]{1,0:T(8,128)(2,1)S(1)}, u32[]{:S(2)}, u32[]{:S(2)}) collective-permute-start(bf16[136,768]{1,0:T(8,128)(2,1)} %get-tuple-element.16.q_ref), channel_id=1, source_target_pairs={{0,2},{1,3},{2,4},{3,5},{4,6},{5,7},{6,8},{7,9},{8,10},{9,11},{10,... | collective-permute-start | bytes 626696 | tf_op jit(solution)/shard_map/ppermute | solution.py:225
  6.7 17.3 %collective-permute-start.2 = (bf16[136,768]{1,0:T(8,128)(2,1)}, bf16[136,768]{1,0:T(8,128)(2,1)S(1)}, u32[]{:S(2)}, u32[]{:S(2)}) collective-permute-start(bf16[136,768]{1,0:T(8,128)(2,1)} %get-tuple-element.16.q_ref), channel_id=1, source_target_pairs={{0,3},{1,4},{2,5},{3,6},{4,7},{5,8},{6,9},{7,10},{8,11},{9,12},{10... | collective-permute-start | bytes 626696 | tf_op jit(solution)/shard_map/ppermute | solution.py:225
  15.2 14.2 %copy-start = (bf16[136,768]{1,0:T(8,128)(2,1)S(1)}, bf16[136,768]{1,0:T(8,128)(2,1)}, u32[]{:S(2)}) copy-start(bf16[136,768]{1,0:T(8,128)(2,1)} %get-tuple-element.16.q_ref) | copy-start | bytes 626692
  15.2 14.2 %copy-start.1 = (bf16[128,256]{1,0:T(8,128)(2,1)S(1)}, bf16[128,256]{1,0:T(8,128)(2,1)}, u32[]{:S(2)}) copy-start(bf16[128,256]{1,0:T(8,128)(2,1)} %kv_ref.1) | copy-start | bytes 196612
  26.2 8.7 %collective-permute-start.4 = (bf16[136,768]{1,0:T(8,128)(2,1)S(1)}, bf16[136,768]{1,0:T(8,128)(2,1)S(1)}, u32[]{:S(2)}, u32[]{:S(2)}) collective-permute-start(bf16[136,768]{1,0:T(8,128)(2,1)S(1)} %far.1), channel_id=1, source_target_pairs={{0,29},{1,30},{2,31},{3,0},{4,1},{5,2},{6,3},{7,4},{8,5},{9,6},{10... | collective-permute-start | bytes 626696 | tf_op jit(solution)/shard_map/ppermute | solution.py:225
  29.4 9.6 %collective-permute-start.3 = (bf16[136,768]{1,0:T(8,128)(2,1)S(1)}, bf16[136,768]{1,0:T(8,128)(2,1)S(1)}, u32[]{:S(2)}, u32[]{:S(2)}) collective-permute-start(bf16[136,768]{1,0:T(8,128)(2,1)S(1)} %both.1), channel_id=1, source_target_pairs={{0,30},{1,31},{2,0},{3,1},{4,2},{5,3},{6,4},{7,5},{8,6},{9,7},{10,... | collective-permute-start | bytes 626696 | tf_op jit(solution)/shard_map/ppermute | solution.py:225

commit v2 on v1

--- a/solution.py
+++ b/solution.py
@@ -12,7 +12,8 @@
 PAGE = 128
 REACH = 4
 PPO = 8
-LONG = 1
+FAR = 8
+GROUP = 2
 ROWS = 128
 WIDTH = HEADS * HD
 STAT_ROWS = 8
@@ -30,16 +31,29 @@
     return q_ref[ROWS:, tile * PAGE : (tile + 1) * PAGE].astype(jnp.float32)
 
 
-def block_keys(q_ref, pages, block):
-    row, lane = iota(0).astype(jnp.float32), iota(1).astype(jnp.float32)
-    first = row < fact(q_ref, CUT)[:1]
+def segment_lanes(q_ref):
+    cut = fact(q_ref, CUT)[:1]
+    row, lane = iota(0).astype(jnp.float32), iota(1)
+    low = jnp.where(lane == 0, 0.0, cut)
+    high = jnp.where(lane == 0, cut, jnp.where(lane == 1, float(ROWS), 0.0))
+    return jnp.where((row >= low) & (row < high), 1.0, 0.0).astype(jnp.bfloat16)
+
+
+def block_keys(q_ref, pages, block, skip=None):
+    row, lane = iota(0).astype(jnp.float32), iota(1)
     counts = fact(q_ref, block)
-    bias = []
+    if skip is not None:
+        counts = jnp.where(skip, 0.0, counts)
+    keys, values = [], []
+    ones = jnp.ones((PAGE, PAGE), jnp.bfloat16)
     for slot in range(PPO):
         count = counts[slot : slot + 1]
-        bias.append(jnp.where(lane < jnp.where(first, count, -count), 0.0, NEGATIVE))
-    flat = pages[...].reshape(PPO * PAGE, 2 * HD)
-    return flat[:, :HD], flat[:, HD:], jnp.concatenate(bias, 1)
+        count = jnp.where(lane[:1] == 0, count, jnp.where(lane[:1] == 1, -count, float(PAGE)))
+        bias = jnp.where(row < count, 0.0, NEGATIVE).astype(jnp.bfloat16)
+        page = pages[slot]
+        keys.append(jnp.concatenate([page[:, :HD], bias], 1))
+        values.append(jnp.concatenate([page[:, HD:], ones], 1))
+    return jnp.concatenate(keys, 0), jnp.concatenate(values, 0)
 
 
 def pack_kernel(length_hbm, table_hbm, segment_hbm, q_hbm, cache_hbm, out_ref, swap_ref, lengths, table, segments, sems):
@@ -77,14 +91,30 @@
         copy.wait()
 
 
-def attend(query, keys, values, bias):
-    s = lax.dot_general(query, keys, (((1,), (1,)), ((), ())), preferred_element_type=jnp.float32)
-    s = s * SCALE2 + bias
-    top = jnp.max(s, axis=1, keepdims=True)
-    w = jnp.exp2(s - top)
-    total = jnp.sum(w, axis=1, keepdims=True)
-    out = jnp.dot(w.astype(jnp.bfloat16), values, preferred_element_type=jnp.float32)
-    return out, top, total
+def scores(query, keys):
+    return lax.dot_general(query, keys, (((1,), (1,)), ((), ())), preferred_element_type=jnp.float32)
+
+
+def attend(q_ref, keys, values):
+    lanes = segment_lanes(q_ref)
+
+    def group_scores(start):
+        query = [jnp.concatenate([head(q_ref, h), lanes], 1) for h in range(start, start + GROUP)]
+        return scores(jnp.concatenate(query, 0), keys)
+
+    parts = []
+    later = group_scores(0)
+    for start in range(0, HEADS, GROUP):
+        s = later
+        if start + GROUP < HEADS:
+            later = group_scores(start + GROUP)
+        top = jnp.max(s, axis=1, keepdims=True)
+        w = jnp.exp2((s - top) * SCALE2).astype(jnp.bfloat16)
+        out = jnp.dot(w, values, preferred_element_type=jnp.float32)
+        for i in range(GROUP):
+            rows = slice(i * ROWS, (i + 1) * ROWS)
+            parts.append((out[rows, :HD], top[rows] * SCALE2, out[rows, HD:]))
+    return parts
 
 
 def join(a, b):
@@ -108,7 +138,7 @@
 def write_payload(out_ref, parts):
     for h, (o, top, total) in enumerate(parts):
         out_ref[:ROWS, h * HD : (h + 1) * HD] = (o / total).astype(jnp.bfloat16)
-    lse = columns([top + jnp.log2(total) for _, top, total in parts]).T[:STAT_ROWS]
+    lse = columns([top + jnp.log2(total[:, :1]) for _, top, total in parts]).T[:STAT_ROWS]
     left = lse
     for i in range(3):
         term = left.astype(jnp.bfloat16)
@@ -120,7 +150,7 @@
 def write_partial(out_ref, lse_ref, parts):
     for h, (o, _, total) in enumerate(parts):
         out_ref[:, h * HD : (h + 1) * HD] = o / total
-    lse_ref[...] = columns([top + jnp.log2(total) for _, top, total in parts])
+    lse_ref[...] = columns([top + jnp.log2(total[:, :1]) for _, top, total in parts])
 
 
 def payload_lse(ref):
@@ -131,42 +161,36 @@
     return full.T
 
 
-def block_parts(q_ref, pages, block):
-    keys, values, bias = block_keys(q_ref, pages, block)
-    return [attend(head(q_ref, h), keys, values, bias) for h in range(HEADS)]
-
-
 def near_kernel(q_ref, kv_ref, page_ref, out_ref, lse_ref):
-    keys, values, bias = block_keys(q_ref, page_ref, 0)
     row, lane = iota(0), iota(1)
     cut = fact(q_ref, CUT)[:1]
     same = (lane <= row) & ((lane.astype(jnp.float32) >= cut) | (row.astype(jnp.float32) < cut))
-    keys = jnp.concatenate([kv_ref[:, :HD], keys], 0)
-    values = jnp.concatenate([kv_ref[:, HD:], values], 0)
-    bias = jnp.concatenate([jnp.where(same, 0.0, NEGATIVE), bias], 1)
-    write_partial(out_ref, lse_ref, [attend(head(q_ref, h), keys, values, bias) for h in range(HEADS)])
+    bias = jnp.where(same, 0.0, NEGATIVE)
+    parts = attend(q_ref, *block_keys(q_ref, page_ref, 0))
+    values = jnp.concatenate([kv_ref[:, HD:], jnp.ones((ROWS, HD), jnp.bfloat16)], 1)
+    for h in range(HEADS):
+        s = scores(head(q_ref, h), kv_ref[:, :HD]) + bias
+        top = jnp.max(s, axis=1, keepdims=True)
+        w = jnp.exp2((s - top) * SCALE2).astype(jnp.bfloat16)
+        out = jnp.dot(w, values, preferred_element_type=jnp.float32)
+        parts[h] = join(parts[h], (out[:, :HD], top * SCALE2, out[:, HD:]))
+    write_partial(out_ref, lse_ref, parts)
 
 
 def far_kernel(q_ref, page_ref, out_ref):
-    write_payload(out_ref, block_parts(q_ref, page_ref, 3))
-
-
-def middle_kernel(q_ref, page_ref, out_ref, lse_ref):
-    write_partial(out_ref, lse_ref, block_parts(q_ref, page_ref, 2))
+    write_payload(out_ref, attend(q_ref, *block_keys(q_ref, page_ref, 3)))
 
 
 def swap_parts(parity, q_ref, swap_ref, part_ref, part_lse_ref):
-    keys, values, bias = block_keys(q_ref, swap_ref, 1)
-    bias = bias + jnp.where(fact(q_ref, PARITY)[:1, :1] == parity, 0.0, NEGATIVE)
-    parts = []
-    for h in range(HEADS):
-        part = part_ref[:, h * HD : (h + 1) * HD], part_lse_ref[:, h : h + 1], 1.0
-        parts.append(join(part, attend(head(q_ref, h), keys, values, bias)))
-    return parts
-
-
-def both_kernel(q_ref, swap_ref, part_ref, part_lse_ref, out_ref):
-    write_payload(out_ref, swap_parts(1.0, q_ref, swap_ref, part_ref, part_lse_ref))
+    parts = attend(q_ref, *block_keys(q_ref, swap_ref, 1, fact(q_ref, PARITY) != parity))
+    given = [(part_ref[:, h * HD : (h + 1) * HD], part_lse_ref[:, h : h + 1], 1.0) for h in range(HEADS)]
+    return [join(a, b) for a, b in zip(given, parts)]
+
+
+def middle_kernel(q_ref, page_ref, swap_ref, out_ref):
+    pages = block_keys(q_ref, page_ref, 2)
+    swapped = block_keys(q_ref, swap_ref, 1, fact(q_ref, PARITY) == 0.0)
+    write_payload(out_ref, attend(q_ref, *(jnp.concatenate(both, 0) for both in zip(pages, swapped))))
 
 
 def own_kernel(q_ref, swap_ref, part_ref, part_lse_ref, out_ref, lse_ref):
@@ -242,21 +266,20 @@
             pltpu.SMEM(segment_ids.shape, jnp.int32),
             pltpu.SemaphoreType.DMA((5,)),
         ],
-        compiler_params=pltpu.CompilerParams(vmem_limit_bytes=(65536 - 1700) << 10),
+        compiler_params=pltpu.CompilerParams(vmem_limit_bytes=16 << 20),
         cost_estimate=cost(16),
         name="pack",
-    )(prefix_len, page_table, segment_ids, queries, cache)
+    )(*(pltpu.with_memory_space_constraint(x, pltpu.HBM) for x in (prefix_len, page_table, segment_ids, queries, cache)))
     q3 = shift(packed, 3, count)
-    q2 = shift(packed, 2, count)
     swapped = lax.ppermute(sent1, AXES, [(s, s ^ 1) for s in range(count)])
+    q2 = shift(after(packed, packed), 2, count)
     pool = after(cache, packed)
     blocks = [pool[i * PPO : (i + 1) * PPO] for i in range(REACH)]
 
-    two = call(middle_kernel, "middle", 1024 * LONG, (FULL, LSE), q2, blocks[2])
-    far = call(far_kernel, "far", 1024 * LONG, SENT, q3, after(blocks[3], two[1]))
+    far = call(far_kernel, "far", 1024 * FAR, SENT, q3, blocks[3])
     back3 = shift(far, -3, count)
-    both = call(both_kernel, "both", 1024, SENT, q2, after(swapped, far), *two)
-    back2 = shift(both, -2, count)
+    middle = call(middle_kernel, "middle", 2048, SENT, q2, blocks[2], after(swapped, far))
+    back2 = shift(middle, -2, count)
     near = call(near_kernel, "near", 1152, (FULL, LSE), packed, new_kv, blocks[0])
     own = call(own_kernel, "own", 1024, (FULL, LSE), packed, swapped, *near)
     return call(final_kernel, "final", 16, RESULT, *own, back2, back3)

time: 40.4 us -> 37.1 us (0.918)
  Pallas kernels: 16.4 us -> 9.85 us
  starting transfers between devices: 6.22 us -> 8.91 us
  waiting for transfers between devices: 16.1 us -> 17.9 us
  local copies, waits for them, and re-layouts: 1.47 us -> 0.11 us
    pallas_call x6 -> x5, Pallas kernels: 14.3 us -> 8.52 us  [call(): pl.pallas_call(body, in_specs=[VMEM] * len(arrays), out_specs=jax.tree.ma...]
    ppermute x4, starting transfers between devices: 3.19 us -> 5.88 us  [shift(): lax.ppermute(value, AXES, [(s, (s + steps) % count) for s in range(count)])]
    ppermute x4, waiting for transfers between devices: 16.1 us -> 17.8 us  [shift(): lax.ppermute(value, AXES, [(s, (s + steps) % count) for s in range(count)])]
    slice x1, local copies, waits for them, and re-layouts: 1.46 us -> 0.1 us  [per_device(): blocks = [pool[i * PPO:(i + 1) * PPO] for i in range(REACH)]]
    pallas_call x1, Pallas kernels: 2.08 us -> 1.33 us  [per_device(): pl.pallas_call(pack_kernel, in_specs=[pl.BlockSpec(memory_space=pltpu.HBM...]
  transfers between devices with their start and end apart: 5 -> 5, of which waited for: 3 -> 2; matrix products, arithmetic and copies ran while one was open for 4% -> 0% of each run, Pallas kernels for 32% -> 20%
where the time goes in v2:
time: 37.1 us; the launch traced here: 36.8 us
  waiting for transfers between devices  17.9 us (48%)
  Pallas kernels  9.85 us (27%)
  starting transfers between devices  8.91 us (24%)
    ppermute x4, waiting for transfers between devices, shift(): lax.ppermute(value, AXES, [(s, (s + steps) % count) for s in range(count)])  17.8 us
    pallas_call x5, Pallas kernels, call(): pl.pallas_call(body, in_specs=[VMEM] * len(arrays), out_specs=jax.tree.ma...  8.52 us
    ppermute x4, starting transfers between devices, shift(): lax.ppermute(value, AXES, [(s, (s + steps) % count) for s in range(count)])  5.88 us
    ppermute x1, starting transfers between devices, per_device(): swapped = lax.ppermute(sent1, AXES, [(s, s ^ 1) for s in range(count)])  3.03 us
    pallas_call x1, Pallas kernels, per_device(): pl.pallas_call(pack_kernel, in_specs=[pl.BlockSpec(memory_space=pltpu.HBM...  1.33 us
  transfers between devices with their start and end apart: 5, of which 2 were waited for; matrix products, arithmetic and copies ran while one was open for 0% of the time, Pallas kernels for 20%

profile of v2, /device:TPU:0, one launch (start us, length us, event | category | flops | bytes accessed | tf_op | source)
XLA Modules:
  0.0 36.8 jit_solution(15799372453266739365)
XLA Ops:
  0.0 0.0 copy-start.1
  0.0 1.3 %pack.1 = (bf16[136,768]{1,0:T(8,128)(2,1)S(1)}, bf16[8,128,256]{2,1,0:T(8,128)(2,1)S(1)}) custom-call(s32[2]{0:T(128)} %length_hbm.1, s32[1,32]{1,0:T(1,128)} %table_hbm.1, s32[128]{0:T(128)} %segment_hbm.1, bf16[128,768]{1,0:T(8,128)(2,1)} %q_hbm.1, bf16[32,128,256]{2,1,0:T(8,128)(2,1)} %cache_hbm.1), custom_call_target="tpu_custom_call" | custom-call | flops 6291456 | bytes 401408 | tf_op jit(solution)/shard_map/pack/pallas_call | solution.py:258
  1.3 3.0 %collective-permute-start = (bf16[8,128,256]{2,1,0:T(8,128)(2,1)S(1)}, bf16[8,128,256]{2,1,0:T(8,128)(2,1)S(1)}, u32[]{:S(2)}, u32[]{:S(2)}) collective-permute-start(bf16[8,128,256]{2,1,0:T(8,128)(2,1)S(1)} %get-tuple-element.15), channel_id=1, source_target_pairs={{0,1},{1,0},{2,3},{3,2},{4,5},{5,4},{6,7},{7,6},{8,9},{9,8},{10,11... | collective-permute-start | bytes 1572872 | tf_op jit(solution)/shard_map/ppermute | solution.py:274
  4.4 1.5 %collective-permute-start.2 = (bf16[136,768]{1,0:T(8,128)(2,1)S(1)}, bf16[136,768]{1,0:T(8,128)(2,1)S(1)}, u32[]{:S(2)}, u32[]{:S(2)}) collective-permute-start(bf16[136,768]{1,0:T(8,128)(2,1)S(1)} %get-tuple-element.21.q_ref), channel_id=1, source_target_pairs={{0,3},{1,4},{2,5},{3,6},{4,7},{5,8},{6,9},{7,10},{8,11},{9,12},{10... | collective-permute-start | bytes 626696 | tf_op jit(solution)/shard_map/ppermute | solution.py:249
  5.9 1.6 %collective-permute-start.1 = (bf16[136,768]{1,0:T(8,128)(2,1)S(1)}, bf16[136,768]{1,0:T(8,128)(2,1)S(1)}, u32[]{:S(2)}, u32[]{:S(2)}) collective-permute-start(bf16[136,768]{1,0:T(8,128)(2,1)S(1)} %get-tuple-element.21.q_ref), channel_id=1, source_target_pairs={{0,2},{1,3},{2,4},{3,5},{4,6},{5,7},{6,8},{7,9},{8,10},{9,11},{10,... | collective-permute-start | bytes 626696 | tf_op jit(solution)/shard_map/ppermute | solution.py:249
  7.5 0.0 copy-done.1
  7.5 0.1 fusion
  7.6 15.7 %collective-permute-done.2.q_ref = bf16[136,768]{1,0:T(8,128)(2,1)S(1)} collective-permute-done((bf16[136,768]{1,0:T(8,128)(2,1)S(1)}, bf16[136,768]{1,0:T(8,128)(2,1)S(1)}, u32[]{:S(2)}, u32[]{:S(2)}) %collective-permute-start.2) | collective-permute-done | bytes 208928 | tf_op jit(solution)/shard_map/ppermute | solution.py:249
  23.3 1.6 %far.1 = bf16[136,768]{1,0:T(8,128)(2,1)S(1)} custom-call(bf16[136,768]{1,0:T(8,128)(2,1)S(1)} %collective-permute-done.2.q_ref, bf16[8,128,256]{2,1,0:T(8,128)(2,1)S(1)} %get-tuple-element.23.page_ref), custom_call_target="tpu_custom_call" | custom-call | flops 3221225472 | bytes 4587520 | tf_op jit(solution)/shard_map/far/pallas_call | solution.py:237
  24.8 0.0 copy-start
  24.8 0.1 collective-permute-start.4
  24.9 0.0 collective-permute-done.swap_ref
  24.9 0.0 collective-permute-done.1.q_ref
  24.9 2.4 %middle.1 = bf16[136,768]{1,0:T(8,128)(2,1)S(1)} custom-call(bf16[136,768]{1,0:T(8,128)(2,1)S(1)} %collective-permute-done.1.q_ref, bf16[8,128,256]{2,1,0:T(8,128)(2,1)S(1)} %get-tuple-element.24.page_ref, bf16[8,128,256]{2,1,0:T(8,128)(2,1)S(1)} %collective-permute-done.swap_ref), custom_call_target="tpu_custom_call" | custom-call | flops 805306368 | bytes 1441792 | tf_op jit(solution)/shard_map/middle/pallas_call | solution.py:237
  27.3 2.7 %collective-permute-start.3 = (bf16[136,768]{1,0:T(8,128)(2,1)S(1)}, bf16[136,768]{1,0:T(8,128)(2,1)S(1)}, u32[]{:S(2)}, u32[]{:S(2)}) collective-permute-start(bf16[136,768]{1,0:T(8,128)(2,1)S(1)} %middle.1), channel_id=1, source_target_pairs={{0,30},{1,31},{2,0},{3,1},{4,2},{5,3},{6,4},{7,5},{8,6},{9,7},{10,... | collective-permute-start | bytes 626696 | tf_op jit(solution)/shard_map/ppermute | solution.py:249
  30.1 0.0 copy-done
  30.1 1.7 %near.1 = (f32[128,768]{1,0:T(8,128)S(1)}, f32[128,128]{1,0:T(8,128)S(1)}) custom-call(bf16[136,768]{1,0:T(8,128)(2,1)S(1)} %get-tuple-element.21.q_ref, bf16[128,256]{1,0:T(8,128)(2,1)S(1)} %copy-done, bf16[8,128,256]{2,1,0:T(8,128)(2,1)S(1)} %get-tuple-element.25.page_ref), custom_call_target="tpu_custom_call" | custom-call | flops 452984832 | bytes 983040 | tf_op jit(solution)/shard_map/near/pallas_call | solution.py:237
  31.8 1.6 %own.1 = (f32[128,768]{1,0:T(8,128)S(1)}, f32[128,128]{1,0:T(8,128)S(1)}) custom-call(bf16[136,768]{1,0:T(8,128)(2,1)S(1)} %get-tuple-element.21.q_ref, bf16[8,128,256]{2,1,0:T(8,128)(2,1)S(1)} %collective-permute-done.swap_ref, f32[128,768]{1,0:T(8,128)S(1)} %get-tuple-element.17.part_ref, f32[128,128]{1,0:T(8,128)S(1)} %get-tuple-element.18.part_lse_ref), custom_call_target="tpu_custom_call" | custom-call | flops 402653184 | bytes 917504 | tf_op jit(solution)/shard_map/own/pallas_call | solution.py:237
  33.3 0.0 collective-permute-done.4.three_ref
  33.4 2.2 %collective-permute-done.3.two_ref = bf16[136,768]{1,0:T(8,128)(2,1)S(1)} collective-permute-done((bf16[136,768]{1,0:T(8,128)(2,1)S(1)}, bf16[136,768]{1,0:T(8,128)(2,1)S(1)}, u32[]{:S(2)}, u32[]{:S(2)}) %collective-permute-start.3) | collective-permute-done | bytes 208928 | tf_op jit(solution)/shard_map/ppermute | solution.py:249
  35.5 1.2 %final.1 = bf16[128,768]{1,0:T(8,128)(2,1)} custom-call(f32[128,768]{1,0:T(8,128)S(1)} %get-tuple-element.19.own_ref, f32[128,128]{1,0:T(8,128)S(1)} %get-tuple-element.20.own_lse_ref, bf16[136,768]{1,0:T(8,128)(2,1)S(1)} %collective-permute-done.3.two_ref, bf16[136,768]{1,0:T(8,128)(2,1)S(1)} %collective-permute-done.4.three_ref), custom_call_target="tpu_custom_call" | custom-call | flops 6291456 | bytes 401408 | tf_op jit(solution)/shard_map/final/pallas_call | solution.py:237
Async XLA Ops:
  0.0 7.5 %copy-start.1 = (bf16[32,128,256]{2,1,0:T(8,128)(2,1)S(1)}, bf16[32,128,256]{2,1,0:T(8,128)(2,1)}, u32[]{:S(2)}) copy-start(bf16[32,128,256]{2,1,0:T(8,128)(2,1)} %cache_hbm.1) | copy-start | bytes 6291460
  1.3 23.6 %collective-permute-start = (bf16[8,128,256]{2,1,0:T(8,128)(2,1)S(1)}, bf16[8,128,256]{2,1,0:T(8,128)(2,1)S(1)}, u32[]{:S(2)}, u32[]{:S(2)}) collective-permute-start(bf16[8,128,256]{2,1,0:T(8,128)(2,1)S(1)} %get-tuple-element.15), channel_id=1, source_target_pairs={{0,1},{1,0},{2,3},{3,2},{4,5},{5,4},{6,7},{7,6},{8,9},{9,8},{10,11... | collective-permute-start | bytes 1572872 | tf_op jit(solution)/shard_map/ppermute | solution.py:274
  4.4 18.9 %collective-permute-start.2 = (bf16[136,768]{1,0:T(8,128)(2,1)S(1)}, bf16[136,768]{1,0:T(8,128)(2,1)S(1)}, u32[]{:S(2)}, u32[]{:S(2)}) collective-permute-start(bf16[136,768]{1,0:T(8,128)(2,1)S(1)} %get-tuple-element.21.q_ref), channel_id=1, source_target_pairs={{0,3},{1,4},{2,5},{3,6},{4,7},{5,8},{6,9},{7,10},{8,11},{9,12},{10... | collective-permute-start | bytes 626696 | tf_op jit(solution)/shard_map/ppermute | solution.py:249
  5.9 19.0 %collective-permute-start.1 = (bf16[136,768]{1,0:T(8,128)(2,1)S(1)}, bf16[136,768]{1,0:T(8,128)(2,1)S(1)}, u32[]{:S(2)}, u32[]{:S(2)}) collective-permute-start(bf16[136,768]{1,0:T(8,128)(2,1)S(1)} %get-tuple-element.21.q_ref), channel_id=1, source_target_pairs={{0,2},{1,3},{2,4},{3,5},{4,6},{5,7},{6,8},{7,9},{8,10},{9,11},{10,... | collective-permute-start | bytes 626696 | tf_op jit(solution)/shard_map/ppermute | solution.py:249
  24.8 5.2 %copy-start = (bf16[128,256]{1,0:T(8,128)(2,1)S(1)}, bf16[128,256]{1,0:T(8,128)(2,1)}, u32[]{:S(2)}) copy-start(bf16[128,256]{1,0:T(8,128)(2,1)} %kv_ref.1) | copy-start | bytes 196612
  24.8 8.5 %collective-permute-start.4 = (bf16[136,768]{1,0:T(8,128)(2,1)S(1)}, bf16[136,768]{1,0:T(8,128)(2,1)S(1)}, u32[]{:S(2)}, u32[]{:S(2)}) collective-permute-start(bf16[136,768]{1,0:T(8,128)(2,1)S(1)} %far.1), channel_id=1, source_target_pairs={{0,29},{1,30},{2,31},{3,0},{4,1},{5,2},{6,3},{7,4},{8,5},{9,6},{10... | collective-permute-start | bytes 626696 | tf_op jit(solution)/shard_map/ppermute | solution.py:249
  27.3 8.2 %collective-permute-start.3 = (bf16[136,768]{1,0:T(8,128)(2,1)S(1)}, bf16[136,768]{1,0:T(8,128)(2,1)S(1)}, u32[]{:S(2)}, u32[]{:S(2)}) collective-permute-start(bf16[136,768]{1,0:T(8,128)(2,1)S(1)} %middle.1), channel_id=1, source_target_pairs={{0,30},{1,31},{2,0},{3,1},{4,2},{5,3},{6,4},{7,5},{8,6},{9,7},{10,... | collective-permute-start | bytes 626696 | tf_op jit(solution)/shard_map/ppermute | solution.py:249

commit v3 on v2

--- a/solution.py
+++ b/solution.py
@@ -12,7 +12,7 @@
 PAGE = 128
 REACH = 4
 PPO = 8
-FAR = 8
+FAR = 2
 GROUP = 2
 ROWS = 128
 WIDTH = HEADS * HD
@@ -187,10 +187,24 @@
     return [join(a, b) for a, b in zip(given, parts)]
 
 
+def two_kernel(q_ref, page_ref, out_ref, lse_ref):
+    write_partial(out_ref, lse_ref, attend(q_ref, *block_keys(q_ref, page_ref, 2)))
+
+
+def swap_parts(parity, q_ref, swap_ref, part_ref, part_lse_ref):
+    parts = attend(q_ref, *block_keys(q_ref, swap_ref, 1, fact(q_ref, PARITY) != parity))
+    given = [(part_ref[:, h * HD : (h + 1) * HD], part_lse_ref[:, h : h + 1], 1.0) for h in range(HEADS)]
+    return [join(a, b) for a, b in zip(given, parts)]
+
+
 def middle_kernel(q_ref, page_ref, swap_ref, out_ref):
     pages = block_keys(q_ref, page_ref, 2)
     swapped = block_keys(q_ref, swap_ref, 1, fact(q_ref, PARITY) == 0.0)
     write_payload(out_ref, attend(q_ref, *(jnp.concatenate(both, 0) for both in zip(pages, swapped))))
+
+
+def middle_kernel(q_ref, swap_ref, part_ref, part_lse_ref, out_ref):
+    write_payload(out_ref, swap_parts(1.0, q_ref, swap_ref, part_ref, part_lse_ref))
 
 
 def own_kernel(q_ref, swap_ref, part_ref, part_lse_ref, out_ref, lse_ref):
@@ -271,17 +285,19 @@
         name="pack",
     )(*(pltpu.with_memory_space_constraint(x, pltpu.HBM) for x in (prefix_len, page_table, segment_ids, queries, cache)))
     q3 = shift(packed, 3, count)
-    swapped = lax.ppermute(sent1, AXES, [(s, s ^ 1) for s in range(count)])
-    q2 = shift(after(packed, packed), 2, count)
+    odd_gets = lax.ppermute(sent1, AXES, [(s, s + 1) for s in range(0, count, 2)])
     pool = after(cache, packed)
     blocks = [pool[i * PPO : (i + 1) * PPO] for i in range(REACH)]
+    near = call(near_kernel, "near", 8, (FULL, LSE), packed, new_kv, blocks[0])
+    q2 = shift(after(packed, near[1]), 2, count)
+    even_gets = lax.ppermute(after(sent1, near[1]), AXES, [(s + 1, s) for s in range(0, count, 2)])
 
     far = call(far_kernel, "far", 1024 * FAR, SENT, q3, blocks[3])
     back3 = shift(far, -3, count)
-    middle = call(middle_kernel, "middle", 2048, SENT, q2, blocks[2], after(swapped, far))
+    two = call(two_kernel, "two", 1024, (FULL, LSE), q2, after(blocks[2], far))
+    middle = call(middle_kernel, "middle", 1024, SENT, q2, after(odd_gets, two[1]), *two)
     back2 = shift(middle, -2, count)
-    near = call(near_kernel, "near", 1152, (FULL, LSE), packed, new_kv, blocks[0])
-    own = call(own_kernel, "own", 1024, (FULL, LSE), packed, swapped, *near)
+    own = call(own_kernel, "own", 1024, (FULL, LSE), packed, even_gets, *near)
     return call(final_kernel, "final", 16, RESULT, *own, back2, back3)
 
 

time: 37.1 us -> 35.6 us (0.960)
  waiting for transfers between devices: 17.9 us -> 12.9 us
  starting transfers between devices: 8.91 us -> 11.7 us
  Pallas kernels: 9.85 us -> 10.6 us
    ppermute x4, waiting for transfers between devices: 17.8 us -> 7.15 us  [shift(): lax.ppermute(value, AXES, [(s, (s + steps) % count) for s in range(count)])]
    ppermute x1 -> x2, waiting for transfers between devices: 0.01 us -> 5.73 us  [the longest x1 4.34 us: per_device(): lax.ppermute(after(sent1, near[1]), AXES, [(s + 1, s) for s in range(0, c...]
    ppermute x1 -> x2, starting transfers between devices: 3.03 us -> 4.73 us  [the longest x1 3.44 us: per_device(): lax.ppermute(sent1, AXES, [(s, s + 1) for s in range(0, count, 2)])]
    ppermute x4, starting transfers between devices: 5.88 us -> 7.01 us  [shift(): lax.ppermute(value, AXES, [(s, (s + steps) % count) for s in range(count)])]
    pallas_call x5 -> x6, Pallas kernels: 8.52 us -> 9.24 us  [call(): pl.pallas_call(body, in_specs=[VMEM] * len(arrays), out_specs=jax.tree.ma...]
  transfers between devices with their start and end apart: 5 -> 6, of which waited for: 2 -> 5; matrix products, arithmetic and copies ran while one was open for 0% -> 0% of each run, Pallas kernels for 20% -> 23%
where the time goes in v3:
time: 35.6 us; the launch traced here: 35.4 us
  waiting for transfers between devices  12.9 us (36%)
  starting transfers between devices  11.7 us (33%)
  Pallas kernels  10.6 us (30%)
    pallas_call x6, Pallas kernels, call(): pl.pallas_call(body, in_specs=[VMEM] * len(arrays), out_specs=jax.tree.ma...  9.24 us
    ppermute x4, waiting for transfers between devices, shift(): lax.ppermute(value, AXES, [(s, (s + steps) % count) for s in range(count)])  7.15 us
    ppermute x4, starting transfers between devices, shift(): lax.ppermute(value, AXES, [(s, (s + steps) % count) for s in range(count)])  7.01 us
    ppermute x1, waiting for transfers between devices, per_device(): lax.ppermute(after(sent1, near[1]), AXES, [(s + 1, s) for s in range(0, c...  4.34 us
    ppermute x1, starting transfers between devices, per_device(): lax.ppermute(sent1, AXES, [(s, s + 1) for s in range(0, count, 2)])  3.44 us
    ppermute x1, waiting for transfers between devices, per_device(): lax.ppermute(sent1, AXES, [(s, s + 1) for s in range(0, count, 2)])  1.39 us
    pallas_call x1, Pallas kernels, per_device(): pl.pallas_call(pack_kernel, in_specs=[pl.BlockSpec(memory_space=pltpu.HBM...  1.33 us
    ppermute x1, starting transfers between devices, per_device(): lax.ppermute(after(sent1, near[1]), AXES, [(s + 1, s) for s in range(0, c...  1.29 us
  transfers between devices with their start and end apart: 6, of which 5 were waited for; matrix products, arithmetic and copies ran while one was open for 0% of the time, Pallas kernels for 23%

profile of v3, /device:TPU:0, one launch (start us, length us, event | category | flops | bytes accessed | tf_op | source)
XLA Modules:
  0.0 35.4 jit_solution(13325815634452260478)
XLA Ops:
  0.0 0.0 copy-start.1
  0.0 1.3 %pack.1 = (bf16[136,768]{1,0:T(8,128)(2,1)S(1)}, bf16[8,128,256]{2,1,0:T(8,128)(2,1)S(1)}) custom-call(s32[2]{0:T(128)} %length_hbm.1, s32[1,32]{1,0:T(1,128)} %table_hbm.1, s32[128]{0:T(128)} %segment_hbm.1, bf16[128,768]{1,0:T(8,128)(2,1)} %q_hbm.1, bf16[32,128,256]{2,1,0:T(8,128)(2,1)} %cache_hbm.1), custom_call_target="tpu_custom_call" | custom-call | flops 6291456 | bytes 401408 | tf_op jit(solution)/shard_map/pack/pallas_call | solution.py:272
  1.3 0.0 copy-start
  1.4 4.0 %collective-permute-start.3 = (bf16[136,768]{1,0:T(8,128)(2,1)S(1)}, bf16[136,768]{1,0:T(8,128)(2,1)S(1)}, u32[]{:S(2)}, u32[]{:S(2)}) collective-permute-start(bf16[136,768]{1,0:T(8,128)(2,1)S(1)} %get-tuple-element.26.q_ref), channel_id=1, source_target_pairs={{0,3},{1,4},{2,5},{3,6},{4,7},{5,8},{6,9},{7,10},{8,11},{9,12},{10... | collective-permute-start | bytes 626696 | tf_op jit(solution)/shard_map/ppermute | solution.py:263
  5.4 3.4 %collective-permute-start.2 = (bf16[8,128,256]{2,1,0:T(8,128)(2,1)S(1)}, bf16[8,128,256]{2,1,0:T(8,128)(2,1)S(1)}, u32[]{:S(2)}, u32[]{:S(2)}) collective-permute-start(bf16[8,128,256]{2,1,0:T(8,128)(2,1)S(1)} %get-tuple-element.22), channel_id=1, source_target_pairs={{0,1},{2,3},{4,5},{6,7},{8,9},{10,11},{12,13},{14,15},{16,17},{18,... | collective-permute-start | bytes 1572872 | tf_op jit(solution)/shard_map/ppermute | solution.py:288
  8.8 0.0 copy-done.1
  8.9 0.1 fusion
  9.0 0.0 copy-done
  9.0 1.7 %near.1 = (f32[128,768]{1,0:T(8,128)S(1)}, f32[128,128]{1,0:T(8,128)S(1)}) custom-call(bf16[136,768]{1,0:T(8,128)(2,1)S(1)} %get-tuple-element.26.q_ref, bf16[128,256]{1,0:T(8,128)(2,1)S(1)} %copy-done, bf16[8,128,256]{2,1,0:T(8,128)(2,1)S(1)} %get-tuple-element.33.page_ref), custom_call_target="tpu_custom_call" | custom-call | flops 3145728 | bytes 397312 | tf_op jit(solution)/shard_map/near/pallas_call | solution.py:251
  10.6 1.3 %collective-permute-start = (bf16[8,128,256]{2,1,0:T(8,128)(2,1)S(1)}, bf16[8,128,256]{2,1,0:T(8,128)(2,1)S(1)}, u32[]{:S(2)}, u32[]{:S(2)}) collective-permute-start(bf16[8,128,256]{2,1,0:T(8,128)(2,1)S(1)} %get-tuple-element.22), channel_id=1, source_target_pairs={{1,0},{3,2},{5,4},{7,6},{9,8},{11,10},{13,12},{15,14},{17,16},{19,... | collective-permute-start | bytes 1572872 | tf_op jit(solution)/shard_map/ppermute | solution.py:293
  11.9 1.6 %collective-permute-start.1 = (bf16[136,768]{1,0:T(8,128)(2,1)S(1)}, bf16[136,768]{1,0:T(8,128)(2,1)S(1)}, u32[]{:S(2)}, u32[]{:S(2)}) collective-permute-start(bf16[136,768]{1,0:T(8,128)(2,1)S(1)} %get-tuple-element.26.q_ref), channel_id=1, source_target_pairs={{0,2},{1,3},{2,4},{3,5},{4,6},{5,7},{6,8},{7,9},{8,10},{9,11},{10,... | collective-permute-start | bytes 626696 | tf_op jit(solution)/shard_map/ppermute | solution.py:263
  13.6 2.7 %collective-permute-done.3.q_ref = bf16[136,768]{1,0:T(8,128)(2,1)S(1)} collective-permute-done((bf16[136,768]{1,0:T(8,128)(2,1)S(1)}, bf16[136,768]{1,0:T(8,128)(2,1)S(1)}, u32[]{:S(2)}, u32[]{:S(2)}) %collective-permute-start.3) | collective-permute-done | bytes 208928 | tf_op jit(solution)/shard_map/ppermute | solution.py:263
  16.2 1.6 %far.1 = bf16[136,768]{1,0:T(8,128)(2,1)S(1)} custom-call(bf16[136,768]{1,0:T(8,128)(2,1)S(1)} %collective-permute-done.3.q_ref, bf16[8,128,256]{2,1,0:T(8,128)(2,1)S(1)} %get-tuple-element.31.page_ref), custom_call_target="tpu_custom_call" | custom-call | flops 805306368 | bytes 1441792 | tf_op jit(solution)/shard_map/far/pallas_call | solution.py:251
  17.8 0.0 collective-permute-start.5
  17.9 3.9 %collective-permute-done.1.q_ref = bf16[136,768]{1,0:T(8,128)(2,1)S(1)} collective-permute-done((bf16[136,768]{1,0:T(8,128)(2,1)S(1)}, bf16[136,768]{1,0:T(8,128)(2,1)S(1)}, u32[]{:S(2)}, u32[]{:S(2)}) %collective-permute-start.1) | collective-permute-done | bytes 208928 | tf_op jit(solution)/shard_map/ppermute | solution.py:263
  21.8 1.5 %two.1 = (f32[128,768]{1,0:T(8,128)S(1)}, f32[128,128]{1,0:T(8,128)S(1)}) custom-call(bf16[136,768]{1,0:T(8,128)(2,1)S(1)} %collective-permute-done.1.q_ref, bf16[8,128,256]{2,1,0:T(8,128)(2,1)S(1)} %get-tuple-element.27.page_ref), custom_call_target="tpu_custom_call" | custom-call | flops 402653184 | bytes 917504 | tf_op jit(solution)/shard_map/two/pallas_call | solution.py:251
  23.3 1.4 %collective-permute-done.2.swap_ref = bf16[8,128,256]{2,1,0:T(8,128)(2,1)S(1)} collective-permute-done((bf16[8,128,256]{2,1,0:T(8,128)(2,1)S(1)}, bf16[8,128,256]{2,1,0:T(8,128)(2,1)S(1)}, u32[]{:S(2)}, u32[]{:S(2)}) %collective-permute-start.2) | collective-permute-done | bytes 524320 | tf_op jit(solution)/shard_map/ppermute | solution.py:288
  24.7 1.6 %middle.1 = bf16[136,768]{1,0:T(8,128)(2,1)S(1)} custom-call(bf16[136,768]{1,0:T(8,128)(2,1)S(1)} %collective-permute-done.1.q_ref, bf16[8,128,256]{2,1,0:T(8,128)(2,1)S(1)} %collective-permute-done.2.swap_ref, f32[128,768]{1,0:T(8,128)S(1)} %get-tuple-element.30.part_ref, f32[128,128]{1,0:T(8,128)S(1)} %get-tuple-element.28.part_lse_ref), custom_call_target="tpu_custom_call" | custom-call | flops 402653184 | bytes 917504 | tf_op jit(solution)/shard_map/middle/pallas_call | solution.py:251
  26.3 1.3 %collective-permute-start.4 = (bf16[136,768]{1,0:T(8,128)(2,1)S(1)}, bf16[136,768]{1,0:T(8,128)(2,1)S(1)}, u32[]{:S(2)}, u32[]{:S(2)}) collective-permute-start(bf16[136,768]{1,0:T(8,128)(2,1)S(1)} %middle.1), channel_id=1, source_target_pairs={{0,30},{1,31},{2,0},{3,1},{4,2},{5,3},{6,4},{7,5},{8,6},{9,7},{10,... | collective-permute-start | bytes 626696 | tf_op jit(solution)/shard_map/ppermute | solution.py:263
  27.6 4.3 %collective-permute-done.swap_ref = bf16[8,128,256]{2,1,0:T(8,128)(2,1)S(1)} collective-permute-done((bf16[8,128,256]{2,1,0:T(8,128)(2,1)S(1)}, bf16[8,128,256]{2,1,0:T(8,128)(2,1)S(1)}, u32[]{:S(2)}, u32[]{:S(2)}) %collective-permute-start) | collective-permute-done | bytes 524320 | tf_op jit(solution)/shard_map/ppermute | solution.py:293
  31.9 1.6 %own.1 = (f32[128,768]{1,0:T(8,128)S(1)}, f32[128,128]{1,0:T(8,128)S(1)}) custom-call(bf16[136,768]{1,0:T(8,128)(2,1)S(1)} %get-tuple-element.26.q_ref, bf16[8,128,256]{2,1,0:T(8,128)(2,1)S(1)} %collective-permute-done.swap_ref, f32[128,768]{1,0:T(8,128)S(1)} %get-tuple-element.23.part_ref, f32[128,128]{1,0:T(8,128)S(1)} %get-tuple-element.21.part_lse_ref), custom_call_target="tpu_custom_call" | custom-call | flops 402653184 | bytes 917504 | tf_op jit(solution)/shard_map/own/pallas_call | solution.py:251
  33.6 0.0 collective-permute-done.5.three_ref
  33.6 0.6 %collective-permute-done.4.two_ref = bf16[136,768]{1,0:T(8,128)(2,1)S(1)} collective-permute-done((bf16[136,768]{1,0:T(8,128)(2,1)S(1)}, bf16[136,768]{1,0:T(8,128)(2,1)S(1)}, u32[]{:S(2)}, u32[]{:S(2)}) %collective-permute-start.4) | collective-permute-done | bytes 208928 | tf_op jit(solution)/shard_map/ppermute | solution.py:263
  34.2 1.2 %final.1 = bf16[128,768]{1,0:T(8,128)(2,1)} custom-call(f32[128,768]{1,0:T(8,128)S(1)} %get-tuple-element.24.own_ref, f32[128,128]{1,0:T(8,128)S(1)} %get-tuple-element.25.own_lse_ref, bf16[136,768]{1,0:T(8,128)(2,1)S(1)} %collective-permute-done.4.two_ref, bf16[136,768]{1,0:T(8,128)(2,1)S(1)} %collective-permute-done.5.three_ref), custom_call_target="tpu_custom_call" | custom-call | flops 6291456 | bytes 401408 | tf_op jit(solution)/shard_map/final/pallas_call | solution.py:251
Async XLA Ops:
  0.0 8.8 %copy-start.1 = (bf16[32,128,256]{2,1,0:T(8,128)(2,1)S(1)}, bf16[32,128,256]{2,1,0:T(8,128)(2,1)}, u32[]{:S(2)}) copy-start(bf16[32,128,256]{2,1,0:T(8,128)(2,1)} %cache_hbm.1) | copy-start | bytes 6291460
  1.3 7.6 %copy-start = (bf16[128,256]{1,0:T(8,128)(2,1)S(1)}, bf16[128,256]{1,0:T(8,128)(2,1)}, u32[]{:S(2)}) copy-start(bf16[128,256]{1,0:T(8,128)(2,1)} %kv_ref.1) | copy-start | bytes 196612
  1.4 14.9 %collective-permute-start.3 = (bf16[136,768]{1,0:T(8,128)(2,1)S(1)}, bf16[136,768]{1,0:T(8,128)(2,1)S(1)}, u32[]{:S(2)}, u32[]{:S(2)}) collective-permute-start(bf16[136,768]{1,0:T(8,128)(2,1)S(1)} %get-tuple-element.26.q_ref), channel_id=1, source_target_pairs={{0,3},{1,4},{2,5},{3,6},{4,7},{5,8},{6,9},{7,10},{8,11},{9,12},{10... | collective-permute-start | bytes 626696 | tf_op jit(solution)/shard_map/ppermute | solution.py:263
  5.4 19.3 %collective-permute-start.2 = (bf16[8,128,256]{2,1,0:T(8,128)(2,1)S(1)}, bf16[8,128,256]{2,1,0:T(8,128)(2,1)S(1)}, u32[]{:S(2)}, u32[]{:S(2)}) collective-permute-start(bf16[8,128,256]{2,1,0:T(8,128)(2,1)S(1)} %get-tuple-element.22), channel_id=1, source_target_pairs={{0,1},{2,3},{4,5},{6,7},{8,9},{10,11},{12,13},{14,15},{16,17},{18,... | collective-permute-start | bytes 1572872 | tf_op jit(solution)/shard_map/ppermute | solution.py:288
  10.6 21.3 %collective-permute-start = (bf16[8,128,256]{2,1,0:T(8,128)(2,1)S(1)}, bf16[8,128,256]{2,1,0:T(8,128)(2,1)S(1)}, u32[]{:S(2)}, u32[]{:S(2)}) collective-permute-start(bf16[8,128,256]{2,1,0:T(8,128)(2,1)S(1)} %get-tuple-element.22), channel_id=1, source_target_pairs={{1,0},{3,2},{5,4},{7,6},{9,8},{11,10},{13,12},{15,14},{17,16},{19,... | collective-permute-start | bytes 1572872 | tf_op jit(solution)/shard_map/ppermute | solution.py:293
  11.9 9.8 %collective-permute-start.1 = (bf16[136,768]{1,0:T(8,128)(2,1)S(1)}, bf16[136,768]{1,0:T(8,128)(2,1)S(1)}, u32[]{:S(2)}, u32[]{:S(2)}) collective-permute-start(bf16[136,768]{1,0:T(8,128)(2,1)S(1)} %get-tuple-element.26.q_ref), channel_id=1, source_target_pairs={{0,2},{1,3},{2,4},{3,5},{4,6},{5,7},{6,8},{7,9},{8,10},{9,11},{10,... | collective-permute-start | bytes 626696 | tf_op jit(solution)/shard_map/ppermute | solution.py:263
  17.8 15.7 %collective-permute-start.5 = (bf16[136,768]{1,0:T(8,128)(2,1)S(1)}, bf16[136,768]{1,0:T(8,128)(2,1)S(1)}, u32[]{:S(2)}, u32[]{:S(2)}) collective-permute-start(bf16[136,768]{1,0:T(8,128)(2,1)S(1)} %far.1), channel_id=1, source_target_pairs={{0,29},{1,30},{2,31},{3,0},{4,1},{5,2},{6,3},{7,4},{8,5},{9,6},{10... | collective-permute-start | bytes 626696 | tf_op jit(solution)/shard_map/ppermute | solution.py:263
  26.3 7.8 %collective-permute-start.4 = (bf16[136,768]{1,0:T(8,128)(2,1)S(1)}, bf16[136,768]{1,0:T(8,128)(2,1)S(1)}, u32[]{:S(2)}, u32[]{:S(2)}) collective-permute-start(bf16[136,768]{1,0:T(8,128)(2,1)S(1)} %middle.1), channel_id=1, source_target_pairs={{0,30},{1,31},{2,0},{3,1},{4,2},{5,3},{6,4},{7,5},{8,6},{9,7},{10,... | collective-permute-start | bytes 626696 | tf_op jit(solution)/shard_map/ppermute | solution.py:263

commit v4 on v3

--- a/solution.py
+++ b/solution.py
@@ -13,7 +13,7 @@
 REACH = 4
 PPO = 8
 FAR = 2
-GROUP = 2
+GROUP = 3
 ROWS = 128
 WIDTH = HEADS * HD
 STAT_ROWS = 8
@@ -148,9 +148,9 @@
 
 
 def write_partial(out_ref, lse_ref, parts):
-    for h, (o, _, total) in enumerate(parts):
+    for h, (o, top, total) in enumerate(parts):
         out_ref[:, h * HD : (h + 1) * HD] = o / total
-    lse_ref[...] = columns([top + jnp.log2(total[:, :1]) for _, top, total in parts])
+        lse_ref[:, h * HD : (h + 1) * HD] = top + jnp.log2(total)
 
 
 def payload_lse(ref):
@@ -183,7 +183,8 @@
 
 def swap_parts(parity, q_ref, swap_ref, part_ref, part_lse_ref):
     parts = attend(q_ref, *block_keys(q_ref, swap_ref, 1, fact(q_ref, PARITY) != parity))
-    given = [(part_ref[:, h * HD : (h + 1) * HD], part_lse_ref[:, h : h + 1], 1.0) for h in range(HEADS)]
+    spans = [slice(h * HD, (h + 1) * HD) for h in range(HEADS)]
+    given = [(part_ref[:, span], part_lse_ref[:, span], 1.0) for span in spans]
     return [join(a, b) for a, b in zip(given, parts)]
 
 
@@ -193,7 +194,8 @@
 
 def swap_parts(parity, q_ref, swap_ref, part_ref, part_lse_ref):
     parts = attend(q_ref, *block_keys(q_ref, swap_ref, 1, fact(q_ref, PARITY) != parity))
-    given = [(part_ref[:, h * HD : (h + 1) * HD], part_lse_ref[:, h : h + 1], 1.0) for h in range(HEADS)]
+    spans = [slice(h * HD, (h + 1) * HD) for h in range(HEADS)]
+    given = [(part_ref[:, span], part_lse_ref[:, span], 1.0) for span in spans]
     return [join(a, b) for a, b in zip(given, parts)]
 
 
@@ -208,7 +210,10 @@
 
 
 def own_kernel(q_ref, swap_ref, part_ref, part_lse_ref, out_ref, lse_ref):
-    write_partial(out_ref, lse_ref, swap_parts(0.0, q_ref, swap_ref, part_ref, part_lse_ref))
+    parts = swap_parts(0.0, q_ref, swap_ref, part_ref, part_lse_ref)
+    for h, (o, _, total) in enumerate(parts):
+        out_ref[:, h * HD : (h + 1) * HD] = o / total
+    lse_ref[...] = columns([top + jnp.log2(total) for _, top, total in parts])
 
 
 def final_kernel(own_ref, own_lse_ref, two_ref, three_ref, out_ref):
@@ -288,13 +293,13 @@
     odd_gets = lax.ppermute(sent1, AXES, [(s, s + 1) for s in range(0, count, 2)])
     pool = after(cache, packed)
     blocks = [pool[i * PPO : (i + 1) * PPO] for i in range(REACH)]
-    near = call(near_kernel, "near", 8, (FULL, LSE), packed, new_kv, blocks[0])
+    near = call(near_kernel, "near", 8, (FULL, FULL), packed, new_kv, blocks[0])
     q2 = shift(after(packed, near[1]), 2, count)
     even_gets = lax.ppermute(after(sent1, near[1]), AXES, [(s + 1, s) for s in range(0, count, 2)])
 
     far = call(far_kernel, "far", 1024 * FAR, SENT, q3, blocks[3])
     back3 = shift(far, -3, count)
-    two = call(two_kernel, "two", 1024, (FULL, LSE), q2, after(blocks[2], far))
+    two = call(two_kernel, "two", 1024, (FULL, FULL), q2, after(blocks[2], far))
     middle = call(middle_kernel, "middle", 1024, SENT, q2, after(odd_gets, two[1]), *two)
     back2 = shift(middle, -2, count)
     own = call(own_kernel, "own", 1024, (FULL, LSE), packed, even_gets, *near)

time: 35.6 us -> 35.5 us (level)
  Pallas kernels: 10.6 us -> 9.83 us
  waiting for transfers between devices: 12.9 us -> 13.4 us
    pallas_call x6, Pallas kernels: 9.24 us -> 8.5 us  [call(): pl.pallas_call(body, in_specs=[VMEM] * len(arrays), out_specs=jax.tree.ma...]
  transfers between devices with their start and end apart: 6 -> 6, of which waited for: 5 -> 5; matrix products, arithmetic and copies ran while one was open for 0% -> 0% of each run, Pallas kernels for 23% -> 21%
where the time goes in v4:
time: 35.5 us; the launch traced here: 35.3 us
  waiting for transfers between devices  13.4 us (38%)
  starting transfers between devices  11.8 us (33%)
  Pallas kernels  9.83 us (28%)
    pallas_call x6, Pallas kernels, call(): pl.pallas_call(body, in_specs=[VMEM] * len(arrays), out_specs=jax.tree.ma...  8.5 us
    ppermute x4, waiting for transfers between devices, shift(): lax.ppermute(value, AXES, [(s, (s + steps) % count) for s in range(count)])  7.41 us
    ppermute x4, starting transfers between devices, shift(): lax.ppermute(value, AXES, [(s, (s + steps) % count) for s in range(count)])  7.1 us
    ppermute x1, waiting for transfers between devices, per_device(): lax.ppermute(after(sent1, near[1]), AXES, [(s + 1, s) for s in range(0, c...  4.39 us
    ppermute x1, starting transfers between devices, per_device(): lax.ppermute(sent1, AXES, [(s, s + 1) for s in range(0, count, 2)])  3.44 us
    ppermute x1, waiting for transfers between devices, per_device(): lax.ppermute(sent1, AXES, [(s, s + 1) for s in range(0, count, 2)])  1.63 us
    pallas_call x1, Pallas kernels, per_device(): pl.pallas_call(pack_kernel, in_specs=[pl.BlockSpec(memory_space=pltpu.HBM...  1.33 us
    ppermute x1, starting transfers between devices, per_device(): lax.ppermute(after(sent1, near[1]), AXES, [(s + 1, s) for s in range(0, c...  1.29 us
  transfers between devices with their start and end apart: 6, of which 5 were waited for; matrix products, arithmetic and copies ran while one was open for 0% of the time, Pallas kernels for 21%

profile of v4, /device:TPU:0, one launch (start us, length us, event | category | flops | bytes accessed | tf_op | source)
XLA Modules:
  0.0 35.3 jit_solution(13762126921561443940)
XLA Ops:
  0.0 0.0 copy-start.1
  0.0 1.3 %pack.1 = (bf16[136,768]{1,0:T(8,128)(2,1)S(1)}, bf16[8,128,256]{2,1,0:T(8,128)(2,1)S(1)}) custom-call(s32[2]{0:T(128)} %length_hbm.1, s32[1,32]{1,0:T(1,128)} %table_hbm.1, s32[128]{0:T(128)} %segment_hbm.1, bf16[128,768]{1,0:T(8,128)(2,1)} %q_hbm.1, bf16[32,128,256]{2,1,0:T(8,128)(2,1)} %cache_hbm.1), custom_call_target="tpu_custom_call" | custom-call | flops 6291456 | bytes 401408 | tf_op jit(solution)/shard_map/pack/pallas_call | solution.py:277
  1.3 0.0 copy-start
  1.4 4.0 %collective-permute-start.3 = (bf16[136,768]{1,0:T(8,128)(2,1)S(1)}, bf16[136,768]{1,0:T(8,128)(2,1)S(1)}, u32[]{:S(2)}, u32[]{:S(2)}) collective-permute-start(bf16[136,768]{1,0:T(8,128)(2,1)S(1)} %get-tuple-element.26.q_ref), channel_id=1, source_target_pairs={{0,3},{1,4},{2,5},{3,6},{4,7},{5,8},{6,9},{7,10},{8,11},{9,12},{10... | collective-permute-start | bytes 626696 | tf_op jit(solution)/shard_map/ppermute | solution.py:268
  5.4 3.4 %collective-permute-start.2 = (bf16[8,128,256]{2,1,0:T(8,128)(2,1)S(1)}, bf16[8,128,256]{2,1,0:T(8,128)(2,1)S(1)}, u32[]{:S(2)}, u32[]{:S(2)}) collective-permute-start(bf16[8,128,256]{2,1,0:T(8,128)(2,1)S(1)} %get-tuple-element.22), channel_id=1, source_target_pairs={{0,1},{2,3},{4,5},{6,7},{8,9},{10,11},{12,13},{14,15},{16,17},{18,... | collective-permute-start | bytes 1572872 | tf_op jit(solution)/shard_map/ppermute | solution.py:293
  8.8 0.0 copy-done.1
  8.9 0.1 fusion
  9.0 0.0 copy-done
  9.0 1.6 %near.1 = (f32[128,768]{1,0:T(8,128)S(1)}, f32[128,768]{1,0:T(8,128)S(1)}) custom-call(bf16[136,768]{1,0:T(8,128)(2,1)S(1)} %get-tuple-element.26.q_ref, bf16[128,256]{1,0:T(8,128)(2,1)S(1)} %copy-done, bf16[8,128,256]{2,1,0:T(8,128)(2,1)S(1)} %get-tuple-element.33.page_ref), custom_call_target="tpu_custom_call" | custom-call | flops 3145728 | bytes 397312 | tf_op jit(solution)/shard_map/near/pallas_call | solution.py:256
  10.6 1.3 %collective-permute-start = (bf16[8,128,256]{2,1,0:T(8,128)(2,1)S(1)}, bf16[8,128,256]{2,1,0:T(8,128)(2,1)S(1)}, u32[]{:S(2)}, u32[]{:S(2)}) collective-permute-start(bf16[8,128,256]{2,1,0:T(8,128)(2,1)S(1)} %get-tuple-element.22), channel_id=1, source_target_pairs={{1,0},{3,2},{5,4},{7,6},{9,8},{11,10},{13,12},{15,14},{17,16},{19,... | collective-permute-start | bytes 1572872 | tf_op jit(solution)/shard_map/ppermute | solution.py:298
  11.9 1.6 %collective-permute-start.1 = (bf16[136,768]{1,0:T(8,128)(2,1)S(1)}, bf16[136,768]{1,0:T(8,128)(2,1)S(1)}, u32[]{:S(2)}, u32[]{:S(2)}) collective-permute-start(bf16[136,768]{1,0:T(8,128)(2,1)S(1)} %get-tuple-element.26.q_ref), channel_id=1, source_target_pairs={{0,2},{1,3},{2,4},{3,5},{4,6},{5,7},{6,8},{7,9},{8,10},{9,11},{10,... | collective-permute-start | bytes 626696 | tf_op jit(solution)/shard_map/ppermute | solution.py:268
  13.5 2.7 %collective-permute-done.3.q_ref = bf16[136,768]{1,0:T(8,128)(2,1)S(1)} collective-permute-done((bf16[136,768]{1,0:T(8,128)(2,1)S(1)}, bf16[136,768]{1,0:T(8,128)(2,1)S(1)}, u32[]{:S(2)}, u32[]{:S(2)}) %collective-permute-start.3) | collective-permute-done | bytes 208928 | tf_op jit(solution)/shard_map/ppermute | solution.py:268
  16.2 1.5 %far.1 = bf16[136,768]{1,0:T(8,128)(2,1)S(1)} custom-call(bf16[136,768]{1,0:T(8,128)(2,1)S(1)} %collective-permute-done.3.q_ref, bf16[8,128,256]{2,1,0:T(8,128)(2,1)S(1)} %get-tuple-element.31.page_ref), custom_call_target="tpu_custom_call" | custom-call | flops 805306368 | bytes 1441792 | tf_op jit(solution)/shard_map/far/pallas_call | solution.py:256
  17.7 0.0 collective-permute-start.5
  17.8 3.9 %collective-permute-done.1.q_ref = bf16[136,768]{1,0:T(8,128)(2,1)S(1)} collective-permute-done((bf16[136,768]{1,0:T(8,128)(2,1)S(1)}, bf16[136,768]{1,0:T(8,128)(2,1)S(1)}, u32[]{:S(2)}, u32[]{:S(2)}) %collective-permute-start.1) | collective-permute-done | bytes 208928 | tf_op jit(solution)/shard_map/ppermute | solution.py:268
  21.7 1.3 %two.1 = (f32[128,768]{1,0:T(8,128)S(1)}, f32[128,768]{1,0:T(8,128)S(1)}) custom-call(bf16[136,768]{1,0:T(8,128)(2,1)S(1)} %collective-permute-done.1.q_ref, bf16[8,128,256]{2,1,0:T(8,128)(2,1)S(1)} %get-tuple-element.27.page_ref), custom_call_target="tpu_custom_call" | custom-call | flops 402653184 | bytes 917504 | tf_op jit(solution)/shard_map/two/pallas_call | solution.py:256
  23.0 1.6 %collective-permute-done.2.swap_ref = bf16[8,128,256]{2,1,0:T(8,128)(2,1)S(1)} collective-permute-done((bf16[8,128,256]{2,1,0:T(8,128)(2,1)S(1)}, bf16[8,128,256]{2,1,0:T(8,128)(2,1)S(1)}, u32[]{:S(2)}, u32[]{:S(2)}) %collective-permute-start.2) | collective-permute-done | bytes 524320 | tf_op jit(solution)/shard_map/ppermute | solution.py:293
  24.6 1.5 %middle.1 = bf16[136,768]{1,0:T(8,128)(2,1)S(1)} custom-call(bf16[136,768]{1,0:T(8,128)(2,1)S(1)} %collective-permute-done.1.q_ref, bf16[8,128,256]{2,1,0:T(8,128)(2,1)S(1)} %collective-permute-done.2.swap_ref, f32[128,768]{1,0:T(8,128)S(1)} %get-tuple-element.30.part_ref, f32[128,768]{1,0:T(8,128)S(1)} %get-tuple-element.28.part_lse_ref), custom_call_target="tpu_custom_call" | custom-call | flops 402653184 | bytes 917504 | tf_op jit(solution)/shard_map/middle/pallas_call | solution.py:256
  26.2 1.4 %collective-permute-start.4 = (bf16[136,768]{1,0:T(8,128)(2,1)S(1)}, bf16[136,768]{1,0:T(8,128)(2,1)S(1)}, u32[]{:S(2)}, u32[]{:S(2)}) collective-permute-start(bf16[136,768]{1,0:T(8,128)(2,1)S(1)} %middle.1), channel_id=1, source_target_pairs={{0,30},{1,31},{2,0},{3,1},{4,2},{5,3},{6,4},{7,5},{8,6},{9,7},{10,... | collective-permute-start | bytes 626696 | tf_op jit(solution)/shard_map/ppermute | solution.py:268
  27.6 4.4 %collective-permute-done.swap_ref = bf16[8,128,256]{2,1,0:T(8,128)(2,1)S(1)} collective-permute-done((bf16[8,128,256]{2,1,0:T(8,128)(2,1)S(1)}, bf16[8,128,256]{2,1,0:T(8,128)(2,1)S(1)}, u32[]{:S(2)}, u32[]{:S(2)}) %collective-permute-start) | collective-permute-done | bytes 524320 | tf_op jit(solution)/shard_map/ppermute | solution.py:298
  31.9 1.4 %own.1 = (f32[128,768]{1,0:T(8,128)S(1)}, f32[128,128]{1,0:T(8,128)S(1)}) custom-call(bf16[136,768]{1,0:T(8,128)(2,1)S(1)} %get-tuple-element.26.q_ref, bf16[8,128,256]{2,1,0:T(8,128)(2,1)S(1)} %collective-permute-done.swap_ref, f32[128,768]{1,0:T(8,128)S(1)} %get-tuple-element.23.part_ref, f32[128,768]{1,0:T(8,128)S(1)} %get-tuple-element.21.part_lse_ref), custom_call_target="tpu_custom_call" | custom-call | flops 402653184 | bytes 917504 | tf_op jit(solution)/shard_map/own/pallas_call | solution.py:256
  33.3 0.0 collective-permute-done.5.three_ref
  33.3 0.8 %collective-permute-done.4.two_ref = bf16[136,768]{1,0:T(8,128)(2,1)S(1)} collective-permute-done((bf16[136,768]{1,0:T(8,128)(2,1)S(1)}, bf16[136,768]{1,0:T(8,128)(2,1)S(1)}, u32[]{:S(2)}, u32[]{:S(2)}) %collective-permute-start.4) | collective-permute-done | bytes 208928 | tf_op jit(solution)/shard_map/ppermute | solution.py:268
  34.1 1.2 %final.1 = bf16[128,768]{1,0:T(8,128)(2,1)} custom-call(f32[128,768]{1,0:T(8,128)S(1)} %get-tuple-element.24.own_ref, f32[128,128]{1,0:T(8,128)S(1)} %get-tuple-element.25.own_lse_ref, bf16[136,768]{1,0:T(8,128)(2,1)S(1)} %collective-permute-done.4.two_ref, bf16[136,768]{1,0:T(8,128)(2,1)S(1)} %collective-permute-done.5.three_ref), custom_call_target="tpu_custom_call" | custom-call | flops 6291456 | bytes 401408 | tf_op jit(solution)/shard_map/final/pallas_call | solution.py:256
Async XLA Ops:
  0.0 8.8 %copy-start.1 = (bf16[32,128,256]{2,1,0:T(8,128)(2,1)S(1)}, bf16[32,128,256]{2,1,0:T(8,128)(2,1)}, u32[]{:S(2)}) copy-start(bf16[32,128,256]{2,1,0:T(8,128)(2,1)} %cache_hbm.1) | copy-start | bytes 6291460
  1.3 7.7 %copy-start = (bf16[128,256]{1,0:T(8,128)(2,1)S(1)}, bf16[128,256]{1,0:T(8,128)(2,1)}, u32[]{:S(2)}) copy-start(bf16[128,256]{1,0:T(8,128)(2,1)} %kv_ref.1) | copy-start | bytes 196612
  1.4 14.9 %collective-permute-start.3 = (bf16[136,768]{1,0:T(8,128)(2,1)S(1)}, bf16[136,768]{1,0:T(8,128)(2,1)S(1)}, u32[]{:S(2)}, u32[]{:S(2)}) collective-permute-start(bf16[136,768]{1,0:T(8,128)(2,1)S(1)} %get-tuple-element.26.q_ref), channel_id=1, source_target_pairs={{0,3},{1,4},{2,5},{3,6},{4,7},{5,8},{6,9},{7,10},{8,11},{9,12},{10... | collective-permute-start | bytes 626696 | tf_op jit(solution)/shard_map/ppermute | solution.py:268
  5.4 19.2 %collective-permute-start.2 = (bf16[8,128,256]{2,1,0:T(8,128)(2,1)S(1)}, bf16[8,128,256]{2,1,0:T(8,128)(2,1)S(1)}, u32[]{:S(2)}, u32[]{:S(2)}) collective-permute-start(bf16[8,128,256]{2,1,0:T(8,128)(2,1)S(1)} %get-tuple-element.22), channel_id=1, source_target_pairs={{0,1},{2,3},{4,5},{6,7},{8,9},{10,11},{12,13},{14,15},{16,17},{18,... | collective-permute-start | bytes 1572872 | tf_op jit(solution)/shard_map/ppermute | solution.py:293
  10.6 21.4 %collective-permute-start = (bf16[8,128,256]{2,1,0:T(8,128)(2,1)S(1)}, bf16[8,128,256]{2,1,0:T(8,128)(2,1)S(1)}, u32[]{:S(2)}, u32[]{:S(2)}) collective-permute-start(bf16[8,128,256]{2,1,0:T(8,128)(2,1)S(1)} %get-tuple-element.22), channel_id=1, source_target_pairs={{1,0},{3,2},{5,4},{7,6},{9,8},{11,10},{13,12},{15,14},{17,16},{19,... | collective-permute-start | bytes 1572872 | tf_op jit(solution)/shard_map/ppermute | solution.py:298
  11.9 9.8 %collective-permute-start.1 = (bf16[136,768]{1,0:T(8,128)(2,1)S(1)}, bf16[136,768]{1,0:T(8,128)(2,1)S(1)}, u32[]{:S(2)}, u32[]{:S(2)}) collective-permute-start(bf16[136,768]{1,0:T(8,128)(2,1)S(1)} %get-tuple-element.26.q_ref), channel_id=1, source_target_pairs={{0,2},{1,3},{2,4},{3,5},{4,6},{5,7},{6,8},{7,9},{8,10},{9,11},{10,... | collective-permute-start | bytes 626696 | tf_op jit(solution)/shard_map/ppermute | solution.py:268
  17.7 15.6 %collective-permute-start.5 = (bf16[136,768]{1,0:T(8,128)(2,1)S(1)}, bf16[136,768]{1,0:T(8,128)(2,1)S(1)}, u32[]{:S(2)}, u32[]{:S(2)}) collective-permute-start(bf16[136,768]{1,0:T(8,128)(2,1)S(1)} %far.1), channel_id=1, source_target_pairs={{0,29},{1,30},{2,31},{3,0},{4,1},{5,2},{6,3},{7,4},{8,5},{9,6},{10... | collective-permute-start | bytes 626696 | tf_op jit(solution)/shard_map/ppermute | solution.py:268
  26.2 7.9 %collective-permute-start.4 = (bf16[136,768]{1,0:T(8,128)(2,1)S(1)}, bf16[136,768]{1,0:T(8,128)(2,1)S(1)}, u32[]{:S(2)}, u32[]{:S(2)}) collective-permute-start(bf16[136,768]{1,0:T(8,128)(2,1)S(1)} %middle.1), channel_id=1, source_target_pairs={{0,30},{1,31},{2,0},{3,1},{4,2},{5,3},{6,4},{7,5},{8,6},{9,7},{10,... | collective-permute-start | bytes 626696 | tf_op jit(solution)/shard_map/ppermute | solution.py:268

commit v5 on v4

--- a/solution.py
+++ b/solution.py
@@ -199,14 +199,18 @@
     return [join(a, b) for a, b in zip(given, parts)]
 
 
-def middle_kernel(q_ref, page_ref, swap_ref, out_ref):
-    pages = block_keys(q_ref, page_ref, 2)
-    swapped = block_keys(q_ref, swap_ref, 1, fact(q_ref, PARITY) == 0.0)
-    write_payload(out_ref, attend(q_ref, *(jnp.concatenate(both, 0) for both in zip(pages, swapped))))
-
-
 def middle_kernel(q_ref, swap_ref, part_ref, part_lse_ref, out_ref):
-    write_payload(out_ref, swap_parts(1.0, q_ref, swap_ref, part_ref, part_lse_ref))
+    odd = jnp.bitwise_and(lax.axis_index("kv"), 1) == 1
+
+    @pl.when(odd)
+    def _():
+        write_payload(out_ref, swap_parts(1.0, q_ref, swap_ref, part_ref, part_lse_ref))
+
+    @pl.when(jnp.logical_not(odd))
+    def _():
+        spans = [slice(h * HD, (h + 1) * HD) for h in range(HEADS)]
+        one = jnp.ones((ROWS, HD), jnp.float32)
+        write_payload(out_ref, [(part_ref[:, span], part_lse_ref[:, span][:, :1], one) for span in spans])
 
 
 def own_kernel(q_ref, swap_ref, part_ref, part_lse_ref, out_ref, lse_ref):

time: 35.5 us -> 35.5 us (level)
  waiting for transfers between devices: 13.4 us -> 14.8 us
  Pallas kernels: 9.83 us -> 8.51 us
    ppermute x1, waiting for transfers between devices: 4.39 us -> 5.71 us  [per_device(): lax.ppermute(after(sent1, near[1]), AXES, [(s + 1, s) for s in range(0, c...]
    pallas_call x6, Pallas kernels: 8.5 us -> 7.18 us  [call(): pl.pallas_call(body, in_specs=[VMEM] * len(arrays), out_specs=jax.tree.ma...]
  transfers between devices with their start and end apart: 6 -> 6, of which waited for: 5 -> 5; matrix products, arithmetic and copies ran while one was open for 0% -> 0% of each run, Pallas kernels for 21% -> 17%
where the time goes in v5:
time: 35.5 us; the launch traced here: 35.3 us
  waiting for transfers between devices  14.8 us (42%)
  starting transfers between devices  11.8 us (33%)
  Pallas kernels  8.51 us (24%)
    ppermute x4, waiting for transfers between devices, shift(): lax.ppermute(value, AXES, [(s, (s + steps) % count) for s in range(count)])  7.41 us
    pallas_call x6, Pallas kernels, call(): pl.pallas_call(body, in_specs=[VMEM] * len(arrays), out_specs=jax.tree.ma...  7.18 us
    ppermute x4, starting transfers between devices, shift(): lax.ppermute(value, AXES, [(s, (s + steps) % count) for s in range(count)])  7.09 us
    ppermute x1, waiting for transfers between devices, per_device(): lax.ppermute(after(sent1, near[1]), AXES, [(s + 1, s) for s in range(0, c...  5.71 us
    ppermute x1, starting transfers between devices, per_device(): lax.ppermute(sent1, AXES, [(s, s + 1) for s in range(0, count, 2)])  3.44 us
    ppermute x1, waiting for transfers between devices, per_device(): lax.ppermute(sent1, AXES, [(s, s + 1) for s in range(0, count, 2)])  1.63 us
    pallas_call x1, Pallas kernels, per_device(): pl.pallas_call(pack_kernel, in_specs=[pl.BlockSpec(memory_space=pltpu.HBM...  1.33 us
    ppermute x1, starting transfers between devices, per_device(): lax.ppermute(after(sent1, near[1]), AXES, [(s + 1, s) for s in range(0, c...  1.29 us
  transfers between devices with their start and end apart: 6, of which 5 were waited for; matrix products, arithmetic and copies ran while one was open for 0% of the time, Pallas kernels for 17%

profile of v5, /device:TPU:0, one launch (start us, length us, event | category | flops | bytes accessed | tf_op | source)
XLA Modules:
  0.0 35.3 jit_solution(14811953943345612416)
XLA Ops:
  0.0 0.0 copy-start.1
  0.0 1.3 %pack.1 = (bf16[136,768]{1,0:T(8,128)(2,1)S(1)}, bf16[8,128,256]{2,1,0:T(8,128)(2,1)S(1)}) custom-call(s32[2]{0:T(128)} %length_hbm.1, s32[1,32]{1,0:T(1,128)} %table_hbm.1, s32[128]{0:T(128)} %segment_hbm.1, bf16[128,768]{1,0:T(8,128)(2,1)} %q_hbm.1, bf16[32,128,256]{2,1,0:T(8,128)(2,1)} %cache_hbm.1), custom_call_target="tpu_custom_call" | custom-call | flops 6291456 | bytes 401408 | tf_op jit(solution)/shard_map/pack/pallas_call | solution.py:281
  1.3 0.0 copy-start
  1.4 4.0 %collective-permute-start.3 = (bf16[136,768]{1,0:T(8,128)(2,1)S(1)}, bf16[136,768]{1,0:T(8,128)(2,1)S(1)}, u32[]{:S(2)}, u32[]{:S(2)}) collective-permute-start(bf16[136,768]{1,0:T(8,128)(2,1)S(1)} %get-tuple-element.26.q_ref), channel_id=1, source_target_pairs={{0,3},{1,4},{2,5},{3,6},{4,7},{5,8},{6,9},{7,10},{8,11},{9,12},{10... | collective-permute-start | bytes 626696 | tf_op jit(solution)/shard_map/ppermute | solution.py:272
  5.4 3.4 %collective-permute-start.2 = (bf16[8,128,256]{2,1,0:T(8,128)(2,1)S(1)}, bf16[8,128,256]{2,1,0:T(8,128)(2,1)S(1)}, u32[]{:S(2)}, u32[]{:S(2)}) collective-permute-start(bf16[8,128,256]{2,1,0:T(8,128)(2,1)S(1)} %get-tuple-element.22), channel_id=1, source_target_pairs={{0,1},{2,3},{4,5},{6,7},{8,9},{10,11},{12,13},{14,15},{16,17},{18,... | collective-permute-start | bytes 1572872 | tf_op jit(solution)/shard_map/ppermute | solution.py:297
  8.8 0.0 copy-done.1
  8.9 0.1 fusion
  9.0 0.0 copy-done
  9.0 1.6 %near.1 = (f32[128,768]{1,0:T(8,128)S(1)}, f32[128,768]{1,0:T(8,128)S(1)}) custom-call(bf16[136,768]{1,0:T(8,128)(2,1)S(1)} %get-tuple-element.26.q_ref, bf16[128,256]{1,0:T(8,128)(2,1)S(1)} %copy-done, bf16[8,128,256]{2,1,0:T(8,128)(2,1)S(1)} %get-tuple-element.33.page_ref), custom_call_target="tpu_custom_call" | custom-call | flops 3145728 | bytes 397312 | tf_op jit(solution)/shard_map/near/pallas_call | solution.py:260
  10.6 1.3 %collective-permute-start = (bf16[8,128,256]{2,1,0:T(8,128)(2,1)S(1)}, bf16[8,128,256]{2,1,0:T(8,128)(2,1)S(1)}, u32[]{:S(2)}, u32[]{:S(2)}) collective-permute-start(bf16[8,128,256]{2,1,0:T(8,128)(2,1)S(1)} %get-tuple-element.22), channel_id=1, source_target_pairs={{1,0},{3,2},{5,4},{7,6},{9,8},{11,10},{13,12},{15,14},{17,16},{19,... | collective-permute-start | bytes 1572872 | tf_op jit(solution)/shard_map/ppermute | solution.py:302
  11.9 1.6 %collective-permute-start.1 = (bf16[136,768]{1,0:T(8,128)(2,1)S(1)}, bf16[136,768]{1,0:T(8,128)(2,1)S(1)}, u32[]{:S(2)}, u32[]{:S(2)}) collective-permute-start(bf16[136,768]{1,0:T(8,128)(2,1)S(1)} %get-tuple-element.26.q_ref), channel_id=1, source_target_pairs={{0,2},{1,3},{2,4},{3,5},{4,6},{5,7},{6,8},{7,9},{8,10},{9,11},{10,... | collective-permute-start | bytes 626696 | tf_op jit(solution)/shard_map/ppermute | solution.py:272
  13.5 2.7 %collective-permute-done.3.q_ref = bf16[136,768]{1,0:T(8,128)(2,1)S(1)} collective-permute-done((bf16[136,768]{1,0:T(8,128)(2,1)S(1)}, bf16[136,768]{1,0:T(8,128)(2,1)S(1)}, u32[]{:S(2)}, u32[]{:S(2)}) %collective-permute-start.3) | collective-permute-done | bytes 208928 | tf_op jit(solution)/shard_map/ppermute | solution.py:272
  16.2 1.5 %far.1 = bf16[136,768]{1,0:T(8,128)(2,1)S(1)} custom-call(bf16[136,768]{1,0:T(8,128)(2,1)S(1)} %collective-permute-done.3.q_ref, bf16[8,128,256]{2,1,0:T(8,128)(2,1)S(1)} %get-tuple-element.31.page_ref), custom_call_target="tpu_custom_call" | custom-call | flops 805306368 | bytes 1441792 | tf_op jit(solution)/shard_map/far/pallas_call | solution.py:260
  17.7 0.0 collective-permute-start.5
  17.8 3.9 %collective-permute-done.1.q_ref = bf16[136,768]{1,0:T(8,128)(2,1)S(1)} collective-permute-done((bf16[136,768]{1,0:T(8,128)(2,1)S(1)}, bf16[136,768]{1,0:T(8,128)(2,1)S(1)}, u32[]{:S(2)}, u32[]{:S(2)}) %collective-permute-start.1) | collective-permute-done | bytes 208928 | tf_op jit(solution)/shard_map/ppermute | solution.py:272
  21.7 1.3 %two.1 = (f32[128,768]{1,0:T(8,128)S(1)}, f32[128,768]{1,0:T(8,128)S(1)}) custom-call(bf16[136,768]{1,0:T(8,128)(2,1)S(1)} %collective-permute-done.1.q_ref, bf16[8,128,256]{2,1,0:T(8,128)(2,1)S(1)} %get-tuple-element.27.page_ref), custom_call_target="tpu_custom_call" | custom-call | flops 402653184 | bytes 917504 | tf_op jit(solution)/shard_map/two/pallas_call | solution.py:260
  23.0 1.6 %collective-permute-done.2.swap_ref = bf16[8,128,256]{2,1,0:T(8,128)(2,1)S(1)} collective-permute-done((bf16[8,128,256]{2,1,0:T(8,128)(2,1)S(1)}, bf16[8,128,256]{2,1,0:T(8,128)(2,1)S(1)}, u32[]{:S(2)}, u32[]{:S(2)}) %collective-permute-start.2) | collective-permute-done | bytes 524320 | tf_op jit(solution)/shard_map/ppermute | solution.py:297
  24.6 0.2 middle.1
  24.9 1.4 %collective-permute-start.4 = (bf16[136,768]{1,0:T(8,128)(2,1)S(1)}, bf16[136,768]{1,0:T(8,128)(2,1)S(1)}, u32[]{:S(2)}, u32[]{:S(2)}) collective-permute-start(bf16[136,768]{1,0:T(8,128)(2,1)S(1)} %middle.1), channel_id=1, source_target_pairs={{0,30},{1,31},{2,0},{3,1},{4,2},{5,3},{6,4},{7,5},{8,6},{9,7},{10,... | collective-permute-start | bytes 626696 | tf_op jit(solution)/shard_map/ppermute | solution.py:272
  26.2 5.7 %collective-permute-done.swap_ref = bf16[8,128,256]{2,1,0:T(8,128)(2,1)S(1)} collective-permute-done((bf16[8,128,256]{2,1,0:T(8,128)(2,1)S(1)}, bf16[8,128,256]{2,1,0:T(8,128)(2,1)S(1)}, u32[]{:S(2)}, u32[]{:S(2)}) %collective-permute-start) | collective-permute-done | bytes 524320 | tf_op jit(solution)/shard_map/ppermute | solution.py:302
  31.9 1.4 %own.1 = (f32[128,768]{1,0:T(8,128)S(1)}, f32[128,128]{1,0:T(8,128)S(1)}) custom-call(bf16[136,768]{1,0:T(8,128)(2,1)S(1)} %get-tuple-element.26.q_ref, bf16[8,128,256]{2,1,0:T(8,128)(2,1)S(1)} %collective-permute-done.swap_ref, f32[128,768]{1,0:T(8,128)S(1)} %get-tuple-element.23.part_ref, f32[128,768]{1,0:T(8,128)S(1)} %get-tuple-element.21.part_lse_ref), custom_call_target="tpu_custom_call" | custom-call | flops 402653184 | bytes 917504 | tf_op jit(solution)/shard_map/own/pallas_call | solution.py:260
  33.3 0.0 collective-permute-done.5.three_ref
  33.3 0.8 %collective-permute-done.4.two_ref = bf16[136,768]{1,0:T(8,128)(2,1)S(1)} collective-permute-done((bf16[136,768]{1,0:T(8,128)(2,1)S(1)}, bf16[136,768]{1,0:T(8,128)(2,1)S(1)}, u32[]{:S(2)}, u32[]{:S(2)}) %collective-permute-start.4) | collective-permute-done | bytes 208928 | tf_op jit(solution)/shard_map/ppermute | solution.py:272
  34.1 1.2 %final.1 = bf16[128,768]{1,0:T(8,128)(2,1)} custom-call(f32[128,768]{1,0:T(8,128)S(1)} %get-tuple-element.24.own_ref, f32[128,128]{1,0:T(8,128)S(1)} %get-tuple-element.25.own_lse_ref, bf16[136,768]{1,0:T(8,128)(2,1)S(1)} %collective-permute-done.4.two_ref, bf16[136,768]{1,0:T(8,128)(2,1)S(1)} %collective-permute-done.5.three_ref), custom_call_target="tpu_custom_call" | custom-call | flops 6291456 | bytes 401408 | tf_op jit(solution)/shard_map/final/pallas_call | solution.py:260
Async XLA Ops:
  0.0 8.8 %copy-start.1 = (bf16[32,128,256]{2,1,0:T(8,128)(2,1)S(1)}, bf16[32,128,256]{2,1,0:T(8,128)(2,1)}, u32[]{:S(2)}) copy-start(bf16[32,128,256]{2,1,0:T(8,128)(2,1)} %cache_hbm.1) | copy-start | bytes 6291460
  1.3 7.7 %copy-start = (bf16[128,256]{1,0:T(8,128)(2,1)S(1)}, bf16[128,256]{1,0:T(8,128)(2,1)}, u32[]{:S(2)}) copy-start(bf16[128,256]{1,0:T(8,128)(2,1)} %kv_ref.1) | copy-start | bytes 196612
  1.4 14.9 %collective-permute-start.3 = (bf16[136,768]{1,0:T(8,128)(2,1)S(1)}, bf16[136,768]{1,0:T(8,128)(2,1)S(1)}, u32[]{:S(2)}, u32[]{:S(2)}) collective-permute-start(bf16[136,768]{1,0:T(8,128)(2,1)S(1)} %get-tuple-element.26.q_ref), channel_id=1, source_target_pairs={{0,3},{1,4},{2,5},{3,6},{4,7},{5,8},{6,9},{7,10},{8,11},{9,12},{10... | collective-permute-start | bytes 626696 | tf_op jit(solution)/shard_map/ppermute | solution.py:272
  5.4 19.2 %collective-permute-start.2 = (bf16[8,128,256]{2,1,0:T(8,128)(2,1)S(1)}, bf16[8,128,256]{2,1,0:T(8,128)(2,1)S(1)}, u32[]{:S(2)}, u32[]{:S(2)}) collective-permute-start(bf16[8,128,256]{2,1,0:T(8,128)(2,1)S(1)} %get-tuple-element.22), channel_id=1, source_target_pairs={{0,1},{2,3},{4,5},{6,7},{8,9},{10,11},{12,13},{14,15},{16,17},{18,... | collective-permute-start | bytes 1572872 | tf_op jit(solution)/shard_map/ppermute | solution.py:297
  10.6 21.4 %collective-permute-start = (bf16[8,128,256]{2,1,0:T(8,128)(2,1)S(1)}, bf16[8,128,256]{2,1,0:T(8,128)(2,1)S(1)}, u32[]{:S(2)}, u32[]{:S(2)}) collective-permute-start(bf16[8,128,256]{2,1,0:T(8,128)(2,1)S(1)} %get-tuple-element.22), channel_id=1, source_target_pairs={{1,0},{3,2},{5,4},{7,6},{9,8},{11,10},{13,12},{15,14},{17,16},{19,... | collective-permute-start | bytes 1572872 | tf_op jit(solution)/shard_map/ppermute | solution.py:302
  11.9 9.8 %collective-permute-start.1 = (bf16[136,768]{1,0:T(8,128)(2,1)S(1)}, bf16[136,768]{1,0:T(8,128)(2,1)S(1)}, u32[]{:S(2)}, u32[]{:S(2)}) collective-permute-start(bf16[136,768]{1,0:T(8,128)(2,1)S(1)} %get-tuple-element.26.q_ref), channel_id=1, source_target_pairs={{0,2},{1,3},{2,4},{3,5},{4,6},{5,7},{6,8},{7,9},{8,10},{9,11},{10,... | collective-permute-start | bytes 626696 | tf_op jit(solution)/shard_map/ppermute | solution.py:272
  17.7 15.6 %collective-permute-start.5 = (bf16[136,768]{1,0:T(8,128)(2,1)S(1)}, bf16[136,768]{1,0:T(8,128)(2,1)S(1)}, u32[]{:S(2)}, u32[]{:S(2)}) collective-permute-start(bf16[136,768]{1,0:T(8,128)(2,1)S(1)} %far.1), channel_id=1, source_target_pairs={{0,29},{1,30},{2,31},{3,0},{4,1},{5,2},{6,3},{7,4},{8,5},{9,6},{10... | collective-permute-start | bytes 626696 | tf_op jit(solution)/shard_map/ppermute | solution.py:272
  24.9 9.2 %collective-permute-start.4 = (bf16[136,768]{1,0:T(8,128)(2,1)S(1)}, bf16[136,768]{1,0:T(8,128)(2,1)S(1)}, u32[]{:S(2)}, u32[]{:S(2)}) collective-permute-start(bf16[136,768]{1,0:T(8,128)(2,1)S(1)} %middle.1), channel_id=1, source_target_pairs={{0,30},{1,31},{2,0},{3,1},{4,2},{5,3},{6,4},{7,5},{8,6},{9,7},{10,... | collective-permute-start | bytes 626696 | tf_op jit(solution)/shard_map/ppermute | solution.py:272
